TPU v7x, 256 devices: a whole 4x4x8 slice. The times are simulated.
256 devices in a mesh: dp: 16 (over z, core), expert: 16 (over y, x).
Axes of the slice: x: 4, y: 4, z: 8, core: 2. Of those that a mesh axis runs over, the one named last changes fastest.
Arguments:
- ssm_state: bfloat16 [1024, 16, 4096], P('expert', None, 'dp'), may hold values from -6 to 6
- conv_state: bfloat16 [1024, 3, 4096], P('expert', None, 'dp'), may hold values from -6 to 6
- new_slot: int32 [1024], replicated, may hold values from 0 to 1023, as said below
- conv_input: bfloat16 [1024, 4096], P('expert', 'dp'), may hold values from -6 to 6
- gate_input: bfloat16 [1024, 4096], P('expert', 'dp'), may hold values from -6 to 6
- conv_weight: float32 [4, 4096], P(None, 'dp'), may hold values from -3 to 3
- conv_bias: float32 [4096], P('dp'), may hold values from -3 to 3
- x_proj_weight: bfloat16 [4096, 288], P('dp'), may hold values from -0.09375 to 0.09375
- step_weight: bfloat16 [256, 4096], P(None, 'dp'), may hold values from -0.375 to 0.375
- step_bias: float32 [4096], P('dp'), may hold values from -3 to -0.5
- decay_log: float32 [16, 4096], P(None, 'dp'), may hold values from 0 to 2
- skip_gain: float32 [4096], P('dp'), may hold values from 0.5 to 1.5
- out_proj_weight: bfloat16 [4096, 4096], P('dp', 'expert'), may hold values from -0.09375 to 0.09375
- residual: bfloat16 [1024, 4096], P(None, 'expert'), may hold values from -6 to 6
- norm_gain: float32 [4096], replicated, may hold values from 0.1 to 1.9
- routes: int32 [1024, 2], replicated, may hold values from 0 to 15, all different within a row; in each aligned block of 64 rows (0 to 63, 64 to 127, ...) at most 20 rows name the same one
- gate_weight: float32 [1024, 2], replicated, may hold values from 0.1 to 0.9
- expert_gate: bfloat16 [16, 4096, 7168], P('expert', None, 'dp'), may hold values from -0.09375 to 0.09375
- expert_up: bfloat16 [16, 4096, 7168], P('expert', None, 'dp'), may hold values from -0.09375 to 0.09375
- expert_down: bfloat16 [16, 7168, 4096], P('expert', 'dp'), may hold values from -0.0625 to 0.0625
Outputs:
- ssm_new: bfloat16 [1024, 16, 4096], P('expert', None, 'dp')
- conv_new: bfloat16 [1024, 3, 4096], P('expert', None, 'dp')
- layer_out: bfloat16 [1024, 4096], P(None, 'expert')
Inputs may be any that keep to these rules, and one draw needn't show every extreme that they name: new_slot is a permutation of the 1024 slots; slot s belongs to expert index s // 64. Of the 64 old slots of one expert index, at most 8 get new slots of any one expert index, and exactly 8 those of some expert index; every expert index sends the same multiset of such counts. `routes`: each row names 2 different experts; within each aligned block of 64 rows (the rows of one expert index) no expert is named by more than 20 rows, a bound that some block reaches.
All inputs are finite; a program needn't handle non-finite values.
Results may differ from a plain program's by a relative error of at most 0.012.
Values may be sent and summed in bfloat16 or wider, within the bound.
A program may use at most 128 MiB of HBM per device.

v0:
```python
import jax
import jax.numpy as jnp
from jax import lax
from jax.sharding import PartitionSpec as P


def dp_total(values):
    return lax.psum(values, "dp")


def body(
    ssm_state,
    conv_state,
    new_slot,
    conv_input,
    gate_input,
    conv_weight,
    conv_bias,
    x_proj_weight,
    step_weight,
    step_bias,
    decay_log,
    skip_gain,
    out_proj_weight,
    residual,
    norm_gain,
    routes,
    gate_weight,
    expert_gate,
    expert_up,
    expert_down,
):
    row_count, state_dim, channels = ssm_state.shape
    owners = lax.axis_size("expert")
    own_index = lax.axis_index("expert")
    move_cap = 2 * row_count // owners
    slot_count = owners * move_cap
    my_slots = lax.dynamic_slice_in_dim(new_slot, own_index * row_count, row_count)
    target = my_slots // row_count
    target_hot = (target[:, None] == jnp.arange(owners)[None, :]).astype(jnp.int32)
    earlier = jnp.sum((jnp.cumsum(target_hot, axis=0) - target_hot) * target_hot, axis=1)
    send_slot = target * move_cap + earlier
    send_hot = (jnp.arange(slot_count)[:, None] == send_slot[None, :]).astype(jnp.bfloat16)
    packed_ssm = (
        jnp.dot(send_hot, ssm_state.reshape(row_count, -1), preferred_element_type=jnp.float32)
        .astype(jnp.bfloat16)
        .reshape(owners, move_cap, -1)
    )
    packed_conv = (
        jnp.dot(send_hot, conv_state.reshape(row_count, -1), preferred_element_type=jnp.float32)
        .astype(jnp.bfloat16)
        .reshape(owners, move_cap, -1)
    )
    recv_ssm, recv_conv = (
        lax.all_to_all(packed_ssm, "expert", split_axis=0, concat_axis=0, tiled=True),
        lax.all_to_all(packed_conv, "expert", split_axis=0, concat_axis=0, tiled=True),
    )
    arriving = (new_slot // row_count == own_index).astype(jnp.int32).reshape(owners, row_count)
    arrive_rank = (jnp.cumsum(arriving, axis=1) - arriving).reshape(-1)
    source_ids = jnp.arange(owners * row_count) // row_count
    recv_slot = source_ids * move_cap + arrive_rank
    new_place = new_slot % row_count
    place_rows = (
        (new_place[None, :] == jnp.arange(row_count)[:, None])
        & (arriving.reshape(-1)[None, :] == 1)
    ).astype(jnp.bfloat16)
    place_slots = (recv_slot[:, None] == jnp.arange(slot_count)[None, :]).astype(jnp.bfloat16)
    place_hot = jnp.dot(place_rows, place_slots, preferred_element_type=jnp.float32).astype(
        jnp.bfloat16
    )
    moved_ssm = (
        jnp.dot(place_hot, recv_ssm.reshape(slot_count, -1), preferred_element_type=jnp.float32)
        .astype(jnp.bfloat16)
        .reshape(row_count, state_dim, channels)
    )
    moved_conv = (
        jnp.dot(place_hot, recv_conv.reshape(slot_count, -1), preferred_element_type=jnp.float32)
        .astype(jnp.bfloat16)
        .reshape(row_count, -1, channels)
    )
    window = jnp.concatenate([moved_conv, conv_input[:, None, :]], axis=1)
    conv_new = window[:, 1:, :]
    conv_sum = (
        jnp.sum(window.astype(jnp.float32) * conv_weight[None, :, :], axis=1) + conv_bias[None, :]
    )
    activated = jax.nn.silu(conv_sum).astype(jnp.bfloat16)
    projected = dp_total(jnp.dot(activated, x_proj_weight, preferred_element_type=jnp.float32))
    rank_dim = step_weight.shape[0]
    step_low = projected[:, :rank_dim]
    b_coef = projected[:, rank_dim : rank_dim + state_dim]
    c_coef = projected[:, rank_dim + state_dim :]
    step_norm = (
        step_low * lax.rsqrt(jnp.mean(step_low * step_low, axis=1, keepdims=True) + 1e-06)
    ).astype(jnp.bfloat16)
    step_size = jax.nn.softplus(
        jnp.dot(step_norm, step_weight, preferred_element_type=jnp.float32) + step_bias[None, :]
    )
    act_float = activated.astype(jnp.float32)
    decays = jnp.exp(step_size[:, None, :] * (-jnp.exp(decay_log))[None, :, :])
    states = (
        decays * moved_ssm.astype(jnp.float32)
        + (step_size * act_float)[:, None, :] * b_coef[:, :, None]
    )
    ssm_new = states.astype(jnp.bfloat16)
    gated_out = (
        (jnp.sum(c_coef[:, :, None] * states, axis=1) + skip_gain[None, :] * act_float)
        * jax.nn.silu(gate_input.astype(jnp.float32))
    ).astype(jnp.bfloat16)
    mamba_mix = dp_total(
        jnp.dot(
            lax.all_gather(gated_out, "expert", axis=0, tiled=True),
            out_proj_weight,
            preferred_element_type=jnp.float32,
        )
    )
    stream = (residual.astype(jnp.float32) + mamba_mix).astype(jnp.bfloat16)
    top_count = routes.shape[1]
    width = stream.shape[1]
    capacity = min(row_count, 5 * row_count * top_count // (2 * owners))
    expert_hot = (
        (routes[:, :, None] == jnp.arange(owners)[None, None, :])
        .astype(jnp.int32)
        .reshape(owners, row_count * top_count, owners)
    )
    prior = jnp.sum((jnp.cumsum(expert_hot, axis=1) - expert_hot) * expert_hot, axis=2)
    slot_of = (routes.reshape(owners, row_count * top_count) * capacity + prior).reshape(
        owners, row_count, top_count
    )
    matches = slot_of[:, :, :, None] == jnp.arange(owners * capacity)[None, None, None, :]
    dispatch_hot = (
        jnp.any(matches, axis=2).astype(jnp.bfloat16).reshape(owners, row_count, owners, capacity)
    )
    combine_w = jnp.sum(
        jnp.where(matches, gate_weight.reshape(owners, row_count, top_count)[:, :, :, None], 0.0),
        axis=2,
    ).reshape(owners, row_count, owners, capacity)
    outgoing = jnp.einsum(
        "orec,ord->eocd",
        dispatch_hot,
        stream.reshape(owners, row_count, width),
        preferred_element_type=jnp.float32,
    ).astype(jnp.bfloat16)
    arrived = lax.all_to_all(outgoing, "expert", split_axis=0, concat_axis=3, tiled=True)
    tokens = arrived.reshape(owners * capacity, -1).astype(jnp.float32)
    normed = (
        tokens
        * lax.rsqrt(jnp.mean(tokens * tokens, axis=1, keepdims=True) + 1e-05)
        * norm_gain[None, :]
    ).astype(jnp.bfloat16)
    gate_val = jnp.dot(normed, expert_gate[0], preferred_element_type=jnp.float32)
    up_val = jnp.dot(normed, expert_up[0], preferred_element_type=jnp.float32)
    hidden = (jax.nn.silu(gate_val) * up_val).astype(jnp.bfloat16)
    partial_out = jnp.dot(hidden, expert_down[0], preferred_element_type=jnp.float32).reshape(
        owners, capacity, -1
    )
    summed = dp_total(partial_out)
    returned = lax.all_to_all(
        summed.astype(jnp.bfloat16), "expert", split_axis=2, concat_axis=0, tiled=True
    ).astype(summed.dtype)
    expert_mix = jnp.einsum(
        "orec,eocd->ord",
        combine_w,
        returned.reshape(owners, owners, capacity, width),
        precision=lax.Precision.HIGHEST,
        preferred_element_type=jnp.float32,
    )
    layer_out = (stream.astype(jnp.float32) + expert_mix.reshape(-1, width)).astype(jnp.bfloat16)
    return (ssm_new, conv_new, layer_out)


def solution(mesh):
    in_specs = (
        P("expert", None, "dp"),
        P("expert", None, "dp"),
        P(),
        P("expert", "dp"),
        P("expert", "dp"),
        P(None, "dp"),
        P("dp"),
        P("dp", None),
        P(None, "dp"),
        P("dp"),
        P(None, "dp"),
        P("dp"),
        P("dp", "expert"),
        P(None, "expert"),
        P(),
        P(),
        P(),
        P("expert", None, "dp"),
        P("expert", None, "dp"),
        P("expert", "dp", None),
    )
    out_specs = (P("expert", None, "dp"), P("expert", None, "dp"), P(None, "expert"))
    return jax.shard_map(body, mesh=mesh, in_specs=in_specs, out_specs=out_specs, check_vma=False)
```

profile of v0, /device:TPU:97, one launch (start us, length us, event | category | flops | bytes accessed | tf_op | source)
XLA Modules:
  0.0 587.0 jit_solution(9232045870672755872)
XLA Ops:
  7.2 0.8 and_select_fusion
  8.4 0.8 multiply_add_fusion
  9.1 0.9 copy.107
  10.0 0.9 fusion.30
  10.9 6.9 %all-to-all-start = ((bf16[16,8,768]{2,1,0:T(8,128)(2,1)}), bf16[16,8,768]{2,1,0:T(8,128)(2,1)S(1)}, u32[]{:S(2)}, u32[]{:S(2)}) async-start(bf16[16,8,768]{2,1,0:T(8,128)(2,1)} %fusion.30), calls=%async_computation | async-start | bytes 393216 | tf_op jit(solution)/shard_map/all_to_all | solution.py:56
  17.8 0.7 broadcast_compare_fusion
  18.9 0.7 add_select_fusion.2
  19.6 1.3 copy.108
  20.9 1.4 fusion.3
  22.7 2.3 all-to-all-done
  25.0 4.4 all-to-all-start.1
  29.9 0.8 fusion.63
  30.9 108.3 %all-reduce.4.cloned.1.call-done = f32[64,288]{1,0:T(8,128)} async-done(((f32[64,288]{1,0:T(8,128)}), f32[64,288]{1,0:T(8,128)}) %all-reduce.4.cloned.1.call-update) | async-done | bytes 73744 | tf_op jit(solution)/shard_map/psum | solution.py:8
  139.2 0.9 multiply_reduce_fusion.2
  140.2 0.9 fusion.65
  141.1 1.1 convert_multiply_fusion.4
  142.9 1.3 multiply_reduce_fusion
  144.2 19.4 %all_gather.3 = bf16[1024,256]{1,0:T(8,128)(2,1)S(1)} all-gather(bf16[64,256]{1,0:T(8,128)(2,1)S(1)} %fusion.46), channel_id=1, replica_groups=mesh['dp'=16,'expert'=16] {'expert'}, dimensions={0}, use_global_device_ids=true | all-gather | bytes 557056 | tf_op jit(solution)/shard_map/all_gather | solution.py:111
  163.6 1.3 fusion.66
  165.7 2.8 select_reduce_fusion.1
  168.6 0.7 fusion.11
  169.2 1.3 copy.91
  170.6 109.3 %all-reduce.6.cloned.1.call-done = f32[1024,256]{1,0:T(8,128)} async-done(((f32[1024,256]{1,0:T(8,128)}), f32[1024,256]{1,0:T(8,128)}) %all-reduce.6.cloned.1.call-update) | async-done | bytes 1048592 | tf_op jit(solution)/shard_map/psum | solution.py:8
  279.8 1.3 add_convert_fusion
  281.2 1.0 convert_bitcast_fusion
  282.1 3.0 copy.93
  285.1 6.7 %all-to-all-start.2 = ((bf16[16,16,20,256]{3,1,2,0:T(8,128)(2,1)}), bf16[16,16,20,256]{3,1,2,0:T(8,128)(2,1)S(1)}, u32[]{:S(2)}, u32[]{:S(2)}) async-start(bf16[16,16,20,256]{3,1,2,0:T(8,128)(2,1)} %copy.93), calls=%async_computation.2 | async-start | bytes 5242880 | tf_op jit(solution)/shard_map/all_to_all | solution.py:143
  291.8 41.7 %all-to-all-done.2 = bf16[16,16,20,256]{3,1,2,0:T(8,128)(2,1)S(1)} async-done(((bf16[16,16,20,256]{3,1,2,0:T(8,128)(2,1)}), bf16[16,16,20,256]{3,1,2,0:T(8,128)(2,1)S(1)}, u32[]{:S(2)}, u32[]{:S(2)}) %all-to-all-start.2) | async-done | bytes 2621472 | tf_op jit(solution)/shard_map/all_to_all | solution.py:143
  333.6 0.6 fusion
  334.1 0.8 fusion.14
  334.9 1.5 copy.94
  336.4 1.2 copy.110
  337.6 0.8 copy-done.13
  338.4 1.5 fusion.9
  340.5 1.5 fusion.27
  342.1 5.9 %fusion.5 = f32[16,20,4096]{2,0,1:T(8,128)} fusion(bf16[1,448,4096]{2,1,0:T(8,128)(2,1)} %param.39, bf16[16,20,448]{2,1,0:T(8,128)(2,1)S(1)} %dot_general.52), kind=kOutput, calls=%fused_computation.9 | convolution fusion | flops 1174405120 | bytes 9199616 | tf_op jit(solution)/shard_map/dot_general | solution.py:153
  348.0 74.7 %all-reduce.7 = bf16[16,20,4096]{2,0,1:T(8,128)(2,1)S(1)} all-reduce(f32[16,20,4096]{2,0,1:T(8,128)} %fusion.5), channel_id=1, replica_groups=mesh['dp'=16,'expert'=16] {'dp'}, use_global_device_ids=true, to_apply=%region_13.14 | all-reduce | flops 1310720 | bytes 7864320 | tf_op jit(solution)/shard_map/psum | solution.py:8
  422.7 14.9 %copy.96 = bf16[16,20,4096]{1,0,2:T(8,128)(2,1)} copy(bf16[16,20,4096]{2,0,1:T(8,128)(2,1)S(1)} %all-reduce.7) | data formatting | bytes 5242880 | tf_op jit(solution)/shard_map/convert_element_type | solution.py:158
  437.6 34.7 %reshape.150 = bf16[16,2,40960]{2,1,0:T(2,128)(2,1)} reshape(bf16[4096,16,20]{2,1,0:T(8,128)(2,1)} %bitcast.85) | data formatting | bytes 5242880
  472.3 4.1 all-to-all-start.3
  476.5 2.0 select_reduce_fusion
  478.5 3.1 copy.90
  481.8 0.7 copy.100
  482.4 35.1 %all-to-all-done.3 = bf16[16,2,40960]{2,1,0:T(2,128)(2,1)S(1)} async-done(((bf16[16,2,40960]{2,1,0:T(2,128)(2,1)}), bf16[16,2,40960]{2,1,0:T(2,128)(2,1)S(1)}, u32[]{:S(2)}, u32[]{:S(2)}) %all-to-all-start.3) | async-done | bytes 2621472 | tf_op jit(solution)/shard_map/all_to_all | solution.py:157
  517.5 42.4 %reshape.151 = bf16[4096,16,20]{2,1,0:T(8,128)(2,1)} reshape(bf16[16,2,40960]{2,1,0:T(2,128)(2,1)S(1)} %all-to-all-done.3) | data formatting | bytes 5242880
  559.9 14.0 %copy.98 = bf16[16,20,16,256]{3,2,1,0:T(8,128)(2,1)S(1)} copy(bf16[16,20,16,256]{1,0,3,2:T(8,128)(2,1)} %bitcast.86) | data formatting | bytes 5242880 | tf_op jit(solution)/shard_map/all_to_all | solution.py:157
  573.9 5.3 fusion.15
  579.2 0.9 fusion.32
  (68 shorter events, 4.1 us)
Async XLA Ops:
  7.2 22.8 %copy-start = (bf16[256,288]{0,1:T(8,128)(2,1)S(1)}, bf16[256,288]{0,1:T(8,128)(2,1)}, u32[]{:S(2)}) copy-start(bf16[256,288]{0,1:T(8,128)(2,1)} %param.27) | copy-start | bytes 442372
  7.2 15.1 %copy-start.5 = (bf16[64,256]{1,0:T(8,128)(2,1)S(1)}, bf16[64,256]{1,0:T(8,128)(2,1)}, u32[]{:S(2)}) copy-start(bf16[64,256]{1,0:T(8,128)(2,1)} %param.23) | copy-start | bytes 98308
  10.9 18.7 %copy-start.10 = (f32[4,256]{1,0:T(4,128)S(1)}, f32[4,256]{1,0:T(4,128)}, u32[]{:S(2)}) copy-start(f32[4,256]{1,0:T(4,128)} %param.25) | copy-start | bytes 12292
  10.9 19.0 %copy-start.11 = (f32[256]{0:T(256)S(1)}, f32[256]{0:T(256)}, u32[]{:S(2)}) copy-start(f32[256]{0:T(256)} %param.26) | copy-start | bytes 3076
  10.9 14.1 %all-to-all-start = ((bf16[16,8,768]{2,1,0:T(8,128)(2,1)}), bf16[16,8,768]{2,1,0:T(8,128)(2,1)S(1)}, u32[]{:S(2)}, u32[]{:S(2)}) async-start(bf16[16,8,768]{2,1,0:T(8,128)(2,1)} %fusion.30), calls=%async_computation | async-start | bytes 393216 | tf_op jit(solution)/shard_map/all_to_all | solution.py:56
  19.6 11.3 %copy-start.7 = (f32[16,256]{1,0:T(8,128)S(1)}, f32[16,256]{1,0:T(8,128)}, u32[]{:S(2)}) copy-start(f32[16,256]{1,0:T(8,128)} %param.30) | copy-start | bytes 49156
  19.6 121.5 %copy-start.15 = (bf16[256,256]{1,0:T(8,128)(2,1)S(1)}, bf16[256,256]{1,0:T(8,128)(2,1)}, u32[]{:S(2)}) copy-start(bf16[256,256]{1,0:T(8,128)(2,1)} %param.28) | copy-start | bytes 393220
  19.6 121.5 %copy-start.16 = (f32[256]{0:T(256)S(1)}, f32[256]{0:T(256)}, u32[]{:S(2)}) copy-start(f32[256]{0:T(256)} %param.29) | copy-start | bytes 3076
  25.0 117.2 %all-to-all-start.1 = ((bf16[16,8,4096]{2,1,0:T(8,128)(2,1)}), bf16[16,8,4096]{2,1,0:T(8,128)(2,1)S(1)}, u32[]{:S(2)}, u32[]{:S(2)}) async-start(bf16[16,8,4096]{2,1,0:T(8,128)(2,1)} %fusion.3), calls=%async_computation.1 | async-start | bytes 2097152 | tf_op jit(solution)/shard_map/all_to_all | solution.py:55
  29.4 109.9 %all-reduce.4.cloned.1.call-start = ((), (), s32[]{:S(2)}) async-start(), calls=%async_computation.4 | async-start | bytes 196608 | tf_op jit(solution)/shard_map/psum | solution.py:8
  30.8 249.0 %all-reduce.6.cloned.1.call-start = ((), (), s32[]{:S(2)}) async-start(), calls=%async_computation.5 | async-start | bytes 2097152 | tf_op jit(solution)/shard_map/psum | solution.py:8
  142.2 2.0 copy-start.6
  142.2 2.0 copy-start.12
  142.2 21.4 %copy-start.3 = (bf16[256,256]{1,0:T(8,128)(2,1)S(1)}, bf16[256,256]{1,0:T(8,128)(2,1)}, u32[]{:S(2)}) copy-start(bf16[256,256]{1,0:T(8,128)(2,1)} %param.32) | copy-start | bytes 393220
  142.8 22.1 %copy-start.4 = (s32[1024,2]{0,1:T(2,128)S(1)}, s32[1024,2]{0,1:T(2,128)}, u32[]{:S(2)}) copy-start(s32[1024,2]{0,1:T(2,128)} %param.35) | copy-start | bytes 24580
  144.2 135.6 %copy-start.2 = (bf16[1024,256]{1,0:T(8,128)(2,1)S(1)}, bf16[1024,256]{1,0:T(8,128)(2,1)}, u32[]{:S(2)}) copy-start(bf16[1024,256]{1,0:T(8,128)(2,1)} %param.33) | copy-start | bytes 1572868
  285.1 6.7 %copy-start.8 = (f32[4096]{0:T(1024)S(1)}, f32[4096]{0:T(1024)}, u32[]{:S(2)}) copy-start(f32[4096]{0:T(1024)} %param.34) | copy-start | bytes 49156
  285.1 48.4 %all-to-all-start.2 = ((bf16[16,16,20,256]{3,1,2,0:T(8,128)(2,1)}), bf16[16,16,20,256]{3,1,2,0:T(8,128)(2,1)S(1)}, u32[]{:S(2)}, u32[]{:S(2)}) async-start(bf16[16,16,20,256]{3,1,2,0:T(8,128)(2,1)} %copy.93), calls=%async_computation.2 | async-start | bytes 5242880 | tf_op jit(solution)/shard_map/all_to_all | solution.py:143
  336.4 2.0 copy-start.13
  338.4 2.0 copy-start.14
  472.3 4.1 copy-start.9
  472.3 45.2 %all-to-all-start.3 = ((bf16[16,2,40960]{2,1,0:T(2,128)(2,1)}), bf16[16,2,40960]{2,1,0:T(2,128)(2,1)S(1)}, u32[]{:S(2)}, u32[]{:S(2)}) async-start(bf16[16,2,40960]{2,1,0:T(2,128)(2,1)} %reshape.150), calls=%async_computation.3 | async-start | bytes 5242880 | tf_op jit(solution)/shard_map/all_to_all | solution.py:157
  573.9 6.2 %copy-start.1 = (bf16[256,288]{0,1:T(8,128)(2,1)S(1)}, bf16[256,288]{0,1:T(8,128)(2,1)}, u32[]{:S(2)}) copy-start(bf16[256,288]{0,1:T(8,128)(2,1)} %param.27) | copy-start | bytes 442372
Sparse Core Ops, SparseCore 0:
  33.1 106.0 all-reduce.3
  165.1 114.7 all-reduce.5
where the time goes:
time: 588 us; the launch traced here: 587 us
  waiting for transfers between devices  297 us (51%)
  local copies, waits for them, and re-layouts  123 us (21%)
  blocking collectives  94 us (16%)
  starting transfers between devices  22.1 us (4%)
  matrix products  21.5 us (4%)
  other arithmetic  15.4 us (3%)
  between operations  14.5 us (2%)
    psum x2, waiting for transfers between devices, dp_total(): return lax.psum(values, 'dp')  218 us
    unnamed x41, local copies, waits for them, and re-layouts  82.2 us
    psum x1, blocking collectives, dp_total(): return lax.psum(values, 'dp')  74.7 us
    all_to_all x1, waiting for transfers between devices, body(): lax.all_to_all(outgoing, 'expert', split_axis=0, concat_axis=3, tiled=True)  41.7 us
    all_to_all x1, waiting for transfers between devices, body(): lax.all_to_all(summed.astype(jnp.bfloat16), 'expert', split_axis=2, conca...  35.1 us
    all_gather x1, blocking collectives, body(): lax.all_gather(gated_out, 'expert', axis=0, tiled=True)  19.4 us
    convert_element_type x1, local copies, waits for them, and re-layouts, body(): summed.astype(jnp.bfloat16)  14.9 us
    all_to_all x1, local copies, waits for them, and re-layouts, body(): lax.all_to_all(summed.astype(jnp.bfloat16), 'expert', split_axis=2, conca...  14 us
  transfers between devices with their start and end apart: 6, of which 5 were waited for; matrix products, arithmetic and copies ran while one was open for 4% of the time, Pallas kernels for 0%

commit v1 on v0

v1 whole, which is shorter than its diff:
```python
import functools

import jax
import jax.numpy as jnp
from jax import lax
from jax.experimental import pallas as pl
from jax.experimental.pallas import tpu as pltpu
from jax.sharding import PartitionSpec as P

MESH = pl.DeviceIdType.MESH
F32 = jnp.float32
BF16 = jnp.bfloat16
LANES = 128


def iota(shape, axis):
    return lax.broadcasted_iota(jnp.int32, shape, axis)


def ones_where(mask):
    return jnp.where(mask, 1.0, 0.0)


def dot(a, b):
    return jnp.dot(a, b, preferred_element_type=F32)


def dot_t(a, b):
    return lax.dot_general(a, b, (((1,), (1,)), ((), ())), preferred_element_type=F32)


def silu(v):
    return v / (1.0 + jnp.exp(-v))


def times(lo, hi, step):
    def run(i, carry):
        step(i)
        return carry

    lax.fori_loop(lo, hi, run, 0)


def kernel(
    dims,
    ssm_hbm, conv_ref, slot_ref, cin_ref, gin_ref, cw_ref, cb_ref, xp_ref, sw_ref, sb_ref,
    dl_ref, sg_ref, wo_ref, res_hbm, ng_ref, rt_ref, gw_ref, wg_hbm, wu_hbm, wd_hbm,
    ssm_out, conv_out, layer_out,
    ssm_v, ssm_f, res_v, wg_v, wu_v, wd_v,
    conv_s, conv_r, ssm_s, ssm_r, ssm_o, conv_o,
    proj_s, proj_r, proj_c, proj_g,
    gat, mix_s, mix_b, mix_t, mix_r, stream_v,
    disp_s, xb, xn, acc_g, acc_u, hid, yp, ysib, yrs, yrr, yls, ylr,
    ret_s, ret_r, dhi_v, dlo_v, outg,
    load_sem, cs_sem, cr_sem, ss_sem, sr_sem, store_sem,
    ps_sem, pr_sem, qs_sem, qr_sem, gs_sem, gr_sem,
    ms_sem, mr_sem, bs_sem, br_sem, ds_sem, dr_sem,
    xrs, xrr, xls, xlr, xss, xsr,
    yss_sem, ysr_sem, yrs_sem, yrr_sem, yls_sem, ylr_sem,
    rs_sem, rr_sem, os_sem, or_sem, ts_sem, tr_sem,
):
    NE, NZ, ROWS, MC, CAP = dims
    ND = 2 * NZ
    PC = 2 * CAP
    LW = 2 * ROWS
    NS = dl_ref.shape[0]
    WB = cin_ref.shape[1]
    RK = sw_ref.shape[0]
    D = NE * WB
    HE = NE // 2
    MP = xn.shape[1]
    shift = ROWS.bit_length() - 1
    d = lax.axis_index("dp")
    e = lax.axis_index("expert")
    z = d // 2
    c = d % 2

    def remote(src, dst, ssem, rsem, dev):
        return pltpu.make_async_remote_copy(
            src_ref=src, dst_ref=dst, send_sem=ssem, recv_sem=rsem, device_id=dev, device_id_type=MESH
        )

    barrier = pltpu.get_barrier_semaphore()
    times(1, NE, lambda i: pl.semaphore_signal(barrier, inc=1, device_id=(d, (e + i) % NE), device_id_type=MESH))
    times(1, ND, lambda i: pl.semaphore_signal(barrier, inc=1, device_id=((d + i) % ND, e), device_id_type=MESH))

    row0 = pl.multiple_of(z * LW, LW)
    lane0 = pl.multiple_of(c * LANES, LANES)
    loads = [
        pltpu.make_async_copy(ssm_hbm, ssm_v, load_sem.at[0]),
        pltpu.make_async_copy(res_hbm.at[pl.ds(row0, LW), pl.ds(lane0, LANES)], res_v, load_sem.at[1]),
        pltpu.make_async_copy(wg_hbm, wg_v, load_sem.at[2]),
        pltpu.make_async_copy(wu_hbm, wu_v, load_sem.at[3]),
        pltpu.make_async_copy(wd_hbm, wd_v, load_sem.at[4]),
    ]
    for load in loads:
        load.start()

    mine = slot_ref[pl.ds(e // 2, 1), :]
    mine = jnp.where(e % 2 == 0, mine[:, :ROWS], mine[:, ROWS:])
    target = lax.shift_right_logical(mine, shift)
    target_hot = ones_where(iota((NE, ROWS), 0) == target)
    before = ones_where(iota((ROWS, ROWS), 0) < iota((ROWS, ROWS), 1)).astype(BF16)
    ahead = dot(target_hot.astype(BF16), before)
    earlier = jnp.sum(target_hot * ahead, axis=0, keepdims=True).astype(jnp.int32)
    pack = ones_where(iota((NE * MC, ROWS), 0) == target * MC + earlier).astype(BF16)
    for k in range(3):
        conv_s[:, k] = dot(pack, conv_ref[k]).reshape(NE, MC, WB).astype(BF16)

    pl.semaphore_wait(barrier, NE - 1 + ND - 1)

    def to_experts(src_of, dst, ssem, rsem):
        def one(i):
            p = (e + i) % NE
            remote(src_of(p), dst, ssem.at[i], rsem.at[e], (d, p)).start()

        times(1, NE, one)

    def sent_experts(src_of, dst, ssem, rsem):
        def one(i):
            p = (e + i) % NE
            remote(src_of(p), dst, ssem.at[i], rsem.at[e], (d, p)).wait_send()

        times(1, NE, one)

    def from_experts(dst_of, ssem, rsem):
        def one(i):
            p = (e + NE - i) % NE
            remote(dst_of(p), dst_of(p), ssem.at[i], rsem.at[p], (d, p)).wait_recv()

        times(1, NE, one)

    to_experts(lambda p: conv_s.at[p], conv_r.at[e], cs_sem, cr_sem)
    conv_r[e] = conv_s[e]

    loads[0].wait()
    ssm_f[...] = ssm_v[...].astype(F32)
    for n in range(NS):
        ssm_s[:, n] = dot(pack, ssm_f[:, n, :].astype(BF16)).reshape(NE, MC, WB).astype(BF16)
    to_experts(lambda p: ssm_s.at[p], ssm_r.at[e], ss_sem, sr_sem)
    ssm_r[e] = ssm_s[e]

    slots = slot_ref[...]
    arriving = ones_where(lax.shift_right_logical(slots, shift) == e)
    lane = iota((LW, LW), 1)
    sub = iota((LW, LW), 0)
    before2 = ones_where((sub < lane) & ((sub < ROWS) == (lane < ROWS))).astype(BF16)
    rank = dot(arriving.astype(BF16), before2)
    place = (slots & (ROWS - 1)).astype(F32) + 1.0
    half = iota((NZ, LW), 1) >= ROWS
    to_lane = iota((NZ, NE * MC), 1) - iota((NZ, NE * MC), 0) * (2 * MC)
    spread = jnp.zeros((NZ, NE * MC), F32)
    for h in range(2):
        live = (arriving > 0.0) & (half == bool(h))
        for k in range(MC):
            found = jnp.sum(jnp.where(live & (rank == float(k)), place, 0.0), axis=1, keepdims=True)
            spread = spread + jnp.where(to_lane == h * MC + k, found, 0.0)
    row_of = jnp.sum(spread, axis=0, keepdims=True).astype(jnp.int32) - 1
    unpack = ones_where(iota((ROWS, NE * MC), 0) == row_of).astype(BF16)

    from_experts(lambda p: conv_r.at[p], cs_sem, cr_sem)
    window = []
    for k in range(3):
        got = conv_r[:, k].astype(F32).reshape(NE * MC, WB).astype(BF16)
        window.append(dot(unpack, got))
    conv_o[0] = window[1].astype(BF16)
    conv_o[1] = window[2].astype(BF16)
    conv_o[2] = cin_ref[...]
    window.append(cin_ref[...].astype(F32))
    total = window[0] * cw_ref[0:1, :]
    for k in range(1, 4):
        total = total + window[k] * cw_ref[k : k + 1, :]
    activated = silu(total + cb_ref[...]).astype(BF16)
    act = activated.astype(F32)
    partial = dot_t(activated, xp_ref[...])
    RZ = ROWS // NZ
    proj_s[...] = jnp.zeros_like(proj_s)
    proj_s[:, :, : RK + 2 * NS] = partial.reshape(NZ, RZ, RK + 2 * NS)

    def proj_src(p):
        return proj_s.at[p // 2, :, pl.ds(pl.multiple_of((p % 2) * LANES, LANES), RK)]

    def to_dp(src_of, dst, ssem, rsem):
        def one(i):
            p = (d + i) % ND
            remote(src_of(p), dst, ssem.at[i], rsem.at[d], (p, e)).start()

        times(1, ND, one)

    def sent_dp(src_of, dst, ssem, rsem):
        def one(i):
            p = (d + i) % ND
            remote(src_of(p), dst, ssem.at[i], rsem.at[d], (p, e)).wait_send()

        times(1, ND, one)

    def from_dp(dst_of, ssem, rsem):
        def one(i):
            p = (d + ND - i) % ND
            remote(dst_of(p), dst_of(p), ssem.at[i], rsem.at[p], (p, e)).wait_recv()

        times(1, ND, one)

    to_dp(proj_src, proj_r.at[d], ps_sem, pr_sem)
    proj_r[d] = proj_s[z, :, pl.ds(lane0, RK)]
    store_conv = pltpu.make_async_copy(conv_o, conv_out, store_sem.at[0])
    store_conv.start()

    r0 = rt_ref[0:1, pl.ds(row0, LW)]
    r1 = rt_ref[1:2, pl.ds(row0, LW)]
    g0 = gw_ref[0:1, pl.ds(row0, LW)]
    g1 = gw_ref[1:2, pl.ds(row0, LW)]
    expert_id = iota((NE, LW), 0)
    named = ones_where((expert_id == r0) | (expert_id == r1))
    weight = jnp.where(expert_id == r0, g0, 0.0) + jnp.where(expert_id == r1, g1, 0.0)
    w_hi = weight.astype(BF16).astype(F32)
    w_lo = weight - w_hi
    in_block = dot(named.astype(BF16), before2).astype(jnp.int32)
    seat = in_block + jnp.where(iota((NE, LW), 1) >= ROWS, CAP, 0)
    seat = jnp.where(named > 0.0, seat, -1)
    seat_id = iota((PC, LW), 0)
    rows_d, rows_hi, rows_lo = [], [], []
    for k in range(NE):
        hit = seat_id == seat[k : k + 1, :]
        rows_d.append(jnp.where(hit, 1.0, 0.0))
        rows_hi.append(jnp.where(hit, w_hi[k : k + 1, :], 0.0))
        rows_lo.append(jnp.where(hit, w_lo[k : k + 1, :], 0.0))
    dispatch = jnp.concatenate(rows_d, axis=0).astype(BF16)
    dhi_v[...] = jnp.concatenate(rows_hi, axis=0).T.astype(BF16)
    dlo_v[...] = jnp.concatenate(rows_lo, axis=0).T.astype(BF16)

    from_dp(lambda p: proj_r.at[p], ps_sem, pr_sem)
    summed = proj_r[0]
    for k in range(1, ND):
        summed = summed + proj_r[k]
    proj_c[...] = summed
    to_dp(lambda p: proj_c, proj_g.at[c, z], qs_sem, qr_sem)
    proj_g[c, z] = summed
    from_dp(lambda p: proj_g.at[p % 2, p // 2], qs_sem, qr_sem)
    step_low = proj_g[0].reshape(ROWS, RK)
    coef = proj_g[1][:, :, RK - LANES :].reshape(ROWS, LANES)
    mean = jnp.sum(step_low * step_low, axis=1, keepdims=True) * (1.0 / RK)
    step_norm = (step_low * lax.rsqrt(mean + 1e-06)).astype(BF16)
    pre = dot(step_norm, sw_ref[...]) + sb_ref[...]
    step = jnp.maximum(pre, 0.0) + jnp.log1p(jnp.exp(-jnp.abs(pre)))
    decay = -jnp.exp(dl_ref[...])
    push = step * act

    from_experts(lambda p: ssm_r.at[p], ss_sem, sr_sem)
    y = sg_ref[...] * act
    read = jnp.zeros_like(y)
    for n in range(NS):
        got = ssm_r[:, n].astype(F32).reshape(NE * MC, WB).astype(BF16)
        moved = dot(unpack, got)
        state = jnp.exp(step * decay[n : n + 1, :]) * moved + push * coef[:, n : n + 1]
        ssm_f[:, n, :] = state
        read = read + coef[:, NS + n : NS + n + 1] * state
    gate = gin_ref[...].astype(F32)
    gated = ((read + y) * silu(gate)).astype(BF16)
    gat[e] = gated
    to_experts(lambda p: gat.at[e], gat.at[e], gs_sem, gr_sem)
    ssm_o[...] = ssm_f[...].astype(BF16)
    store_ssm = pltpu.make_async_copy(ssm_o, ssm_out, store_sem.at[1])
    store_ssm.start()

    from_experts(lambda p: gat.at[p], gs_sem, gr_sem)
    for k in range(NZ):
        mixed = dot(gat[2 * k : 2 * k + 2].reshape(LW, WB), wo_ref[...])
        mix_s[0, k] = mixed[:, :LANES].astype(BF16)
        mix_s[1, k] = mixed[:, LANES:].astype(BF16)
    sibling = (2 * z + 1 - c, e)
    mix_swap = remote(mix_s.at[1 - c], mix_b, bs_sem.at[0], br_sem.at[0], sibling)
    mix_swap.start()
    mix_swap.wait_recv()
    for k in range(NZ):
        mix_t[k] = (mix_s[c, k].astype(F32) + mix_b[k].astype(F32)).astype(BF16)

    def send_mix(i):
        p = (z + i) % NZ
        return remote(mix_t.at[p], mix_r.at[z], ms_sem.at[i], mr_sem.at[z], (2 * p + c, e))

    times(1, NZ, lambda i: send_mix(i).start())
    mix_r[z] = mix_t[z]

    def recv_mix(i):
        p = (z + NZ - i) % NZ
        remote(mix_r.at[p], mix_r.at[p], ms_sem.at[i], mr_sem.at[p], (2 * p + c, e)).wait_recv()

    times(1, NZ, recv_mix)
    loads[1].wait()
    mixed = mix_r[0].astype(F32)
    for k in range(1, NZ):
        mixed = mixed + mix_r[k].astype(F32)
    stream = (res_v[...].astype(F32) + mixed).astype(BF16)
    stream_v[...] = stream

    disp_s[...] = dot(dispatch, stream).reshape(NE, PC, LANES).astype(BF16)
    to_experts(lambda p: disp_s.at[p], xb.at[c, z, e], ds_sem, dr_sem)
    xb[c, z, e] = disp_s[e]
    from_experts(lambda p: xb.at[c, z, p], ds_sem, dr_sem)

    right = (2 * ((z + 1) % NZ) + c, e)
    left = (2 * ((z + NZ - 1) % NZ) + c, e)
    far = NZ // 2
    hops_r = (far, NZ - 1 - far)
    hops_l = (NZ - 1 - far, far)
    halves = (pl.ds(0, HE), pl.ds(HE, HE))

    def back(s):
        return (z + NZ - s) % NZ

    def ahead_z(s):
        return (z + s) % NZ

    def ring_right(h, s):
        p = back(s)
        part = xb.at[c, p, halves[h]]
        return remote(part, part, xrs.at[h, s], xrr.at[h, s], right)

    def ring_left(h, s):
        p = ahead_z(s)
        part = xb.at[c, p, halves[h]]
        return remote(part, part, xls.at[h, s], xlr.at[h, s], left)

    def wait_right(h, s):
        part = xb.at[c, back(s + 1), halves[h]]
        remote(part, part, xrs.at[h, s], xrr.at[h, s], right).wait_recv()

    def wait_left(h, s):
        part = xb.at[c, ahead_z(s + 1), halves[h]]
        remote(part, part, xls.at[h, s], xlr.at[h, s], left).wait_recv()

    def over(h, p):
        part = xb.at[c, p, halves[h]]
        return remote(part, part, xss.at[h, p], xsr.at[h, p], sibling)

    def wait_over(h, p):
        part = xb.at[1 - c, p, halves[h]]
        remote(part, part, xss.at[h, p], xsr.at[h, p], sibling).wait_recv()

    def normalise(p):
        square = jnp.zeros((PC, LANES), F32)
        for k in range(NE):
            for m in range(2):
                v = xb[m, p, k].astype(F32)
                square = square + v * v
        scale = lax.rsqrt(jnp.sum(square, axis=1, keepdims=True) * (1.0 / D) + 1e-05)
        for k in range(NE):
            for m in range(2):
                v = xb[m, p, k].astype(F32) * scale * ng_ref[2 * k + m : 2 * k + m + 1, :]
                if MP > PC:
                    v = jnp.concatenate([v, jnp.zeros((MP - PC, LANES), F32)], axis=0)
                xn[p, :, (2 * k + m) * LANES : (2 * k + m + 1) * LANES] = v.astype(BF16)

    for s in range(far):
        for h in range(2):
            if 0 < s <= hops_r[h]:
                wait_right(h, s - 1)
            if s < hops_r[h]:
                ring_right(h, s).start()
            if 0 < s <= hops_l[h]:
                wait_left(h, s - 1)
            if s < hops_l[h]:
                ring_left(h, s).start()
        for p in [z] if s == 0 else [back(s), ahead_z(s)]:
            for h in range(2):
                over(h, p).start()
            for h in range(2):
                wait_over(h, p)
            normalise(p)
    last = ahead_z(far)
    for h in range(2):
        if hops_r[h] == far:
            wait_right(h, far - 1)
        if hops_l[h] == far:
            wait_left(h, far - 1)
        over(h, last).start()
    for h in range(2):
        wait_over(h, last)
    normalise(last)

    loads[2].wait()
    loads[3].wait()
    KC = min(D, 1024)
    acc_g[...] = jnp.zeros_like(acc_g)
    acc_u[...] = jnp.zeros_like(acc_u)

    def depth(k):
        at = pl.ds(pl.multiple_of(k * KC, KC), KC)
        x = xn[:, :, at].reshape(NZ * MP, KC)
        acc_g[...] += dot_t(x, wg_v[:, at])
        acc_u[...] += dot_t(x, wu_v[:, at])

    times(0, D // KC, depth)
    hid[...] = (silu(acc_g[...]) * acc_u[...]).astype(BF16)
    loads[4].wait()

    def down(h, k):
        at = pl.ds(pl.multiple_of((h * HE + k) * WB, WB), WB)
        out = dot(hid[...], wd_v[:, at]).reshape(NZ, MP, WB)[:, :PC].astype(BF16)
        yp[0, h, :, k] = out[:, :, :LANES]
        yp[1, h, :, k] = out[:, :, LANES:]

    def swap_y(h):
        return remote(yp.at[1 - c, h], ysib.at[h], yss_sem.at[h], ysr_sem.at[h], sibling)

    for h in range(2):
        times(0, HE, lambda k: down(h, k))
        swap_y(h).start()

    def own(h, p):
        return yp[c, h, p].astype(F32) + ysib[h, p].astype(F32)

    def chain_right(h, s):
        return remote(yrs.at[h, s], yrr.at[h, s], yrs_sem.at[h, s], yrr_sem.at[h, s], right)

    def chain_left(h, s):
        return remote(yls.at[h, s], ylr.at[h, s], yls_sem.at[h, s], ylr_sem.at[h, s], left)

    for s in range(far):
        for h in range(2):
            if s == 0:
                swap_y(h).wait_recv()
            if s < hops_r[h]:
                part = own(h, ahead_z(hops_r[h] - s))
                if s > 0:
                    chain_right(h, s - 1).wait_recv()
                    part = part + yrr[h, s - 1].astype(F32)
                yrs[h, s] = part.astype(BF16)
                chain_right(h, s).start()
            if s < hops_l[h]:
                part = own(h, back(hops_l[h] - s))
                if s > 0:
                    chain_left(h, s - 1).wait_recv()
                    part = part + ylr[h, s - 1].astype(F32)
                yls[h, s] = part.astype(BF16)
                chain_left(h, s).start()
    for h in range(2):
        part = own(h, z)
        if hops_r[h] > 0:
            chain_right(h, hops_r[h] - 1).wait_recv()
            part = part + yrr[h, hops_r[h] - 1].astype(F32)
        if hops_l[h] > 0:
            chain_left(h, hops_l[h] - 1).wait_recv()
            part = part + ylr[h, hops_l[h] - 1].astype(F32)
        ret_s[h * HE : (h + 1) * HE] = part.astype(BF16)

    to_experts(lambda p: ret_s.at[p], ret_r.at[e], rs_sem, rr_sem)
    ret_r[e] = ret_s[e]
    from_experts(lambda p: ret_r.at[p], rs_sem, rr_sem)
    back_rows = ret_r[...].astype(F32).reshape(NE * PC, LANES).astype(BF16)
    final = stream_v[...].astype(F32) + dot(dhi_v[...], back_rows) + dot(dlo_v[...], back_rows)
    outg[c, z] = final.astype(BF16)

    def send_out(i):
        p = (z + i) % NZ
        return remote(outg.at[c, z], outg.at[c, z], os_sem.at[i], or_sem.at[z], (2 * p + c, e))

    def wait_out(i):
        p = (z + NZ - i) % NZ
        remote(outg.at[c, p], outg.at[c, p], os_sem.at[i], or_sem.at[p], (2 * p + c, e)).wait_recv()

    def pass_out(p):
        return remote(outg.at[c, p], outg.at[c, p], ts_sem.at[p], tr_sem.at[p], sibling)

    times(1, NZ, lambda i: send_out(i).start())
    pass_out(z).start()

    def relay(i):
        wait_out(i)
        pass_out((z + NZ - i) % NZ).start()

    times(1, NZ, relay)

    def wait_pass(p):
        remote(outg.at[1 - c, p], outg.at[1 - c, p], ts_sem.at[p], tr_sem.at[p], sibling).wait_recv()

    times(0, NZ, wait_pass)
    for k in range(NZ):
        for m in range(2):
            layer_out[k * LW : (k + 1) * LW, m * LANES : (m + 1) * LANES] = outg[m, k]

    store_conv.wait()
    store_ssm.wait()
    sent_experts(lambda p: conv_s.at[p], conv_r.at[e], cs_sem, cr_sem)
    sent_experts(lambda p: ssm_s.at[p], ssm_r.at[e], ss_sem, sr_sem)
    sent_dp(proj_src, proj_r.at[d], ps_sem, pr_sem)
    sent_dp(lambda p: proj_c, proj_g.at[c, z], qs_sem, qr_sem)
    sent_experts(lambda p: gat.at[e], gat.at[e], gs_sem, gr_sem)
    mix_swap.wait_send()
    times(1, NZ, lambda i: send_mix(i).wait_send())
    sent_experts(lambda p: disp_s.at[p], xb.at[c, z, e], ds_sem, dr_sem)
    for h in range(2):
        for s in range(hops_r[h]):
            ring_right(h, s).wait_send()
            chain_right(h, s).wait_send()
        for s in range(hops_l[h]):
            ring_left(h, s).wait_send()
            chain_left(h, s).wait_send()
        swap_y(h).wait_send()
        times(0, NZ, lambda p: over(h, p).wait_send())
    sent_experts(lambda p: ret_s.at[p], ret_r.at[e], rs_sem, rr_sem)
    times(1, NZ, lambda i: send_out(i).wait_send())
    times(0, NZ, lambda p: pass_out(p).wait_send())


def body(
    ssm_state, conv_state, new_slot, conv_input, gate_input, conv_weight, conv_bias, x_proj_weight,
    step_weight, step_bias, decay_log, skip_gain, out_proj_weight, residual, norm_gain, routes,
    gate_weight, expert_gate, expert_up, expert_down,
):
    ROWS, NS, WB = ssm_state.shape
    NE = lax.axis_size("expert")
    NZ = lax.axis_size("dp") // 2
    RK = step_weight.shape[0]
    FB = expert_gate.shape[2]
    MC = 2 * ROWS // NE
    CAP = min(ROWS, 5 * ROWS * routes.shape[1] // (2 * NE))
    PC, LW, D, HE = 2 * CAP, 2 * ROWS, NE * WB, NE // 2
    MP = (PC + 15) // 16 * 16
    RZ = ROWS // NZ
    far = NZ // 2
    hbm = pl.BlockSpec(memory_space=pl.ANY)
    vmem = pl.BlockSpec(memory_space=pltpu.VMEM)
    V, S = pltpu.VMEM, pltpu.SemaphoreType.DMA
    scratch = [
        V((ROWS, NS, WB), BF16), V((ROWS, NS, WB), F32), V((LW, LANES), BF16),
        V((FB, D), BF16), V((FB, D), BF16), V((FB, D), BF16),
        V((NE, 3, MC, WB), BF16), V((NE, 3, MC, WB), BF16),
        V((NE, NS, MC, WB), BF16), V((NE, NS, MC, WB), BF16),
        V((ROWS, NS, WB), BF16), V((3, ROWS, WB), BF16),
        V((NZ, RZ, RK + LANES), F32), V((2 * NZ, RZ, RK), F32), V((RZ, RK), F32), V((2, NZ, RZ, RK), F32),
        V((NE, ROWS, WB), BF16), V((2, NZ, LW, LANES), BF16), V((NZ, LW, LANES), BF16),
        V((NZ, LW, LANES), BF16), V((NZ, LW, LANES), BF16), V((LW, LANES), BF16),
        V((NE, PC, LANES), BF16), V((2, NZ, NE, PC, LANES), BF16), V((NZ, MP, D), BF16),
        V((NZ * MP, FB), F32), V((NZ * MP, FB), F32), V((NZ * MP, FB), BF16),
        V((2, 2, NZ, HE, PC, LANES), BF16), V((2, NZ, HE, PC, LANES), BF16),
        V((2, far, HE, PC, LANES), BF16), V((2, far, HE, PC, LANES), BF16),
        V((2, far, HE, PC, LANES), BF16), V((2, far, HE, PC, LANES), BF16),
        V((NE, PC, LANES), BF16), V((NE, PC, LANES), BF16),
        V((LW, NE * PC), BF16), V((LW, NE * PC), BF16), V((2, NZ, LW, LANES), BF16),
        S((5,)), S((NE,)), S((NE,)), S((NE,)), S((NE,)), S((2,)),
        S((2 * NZ,)), S((2 * NZ,)), S((2 * NZ,)), S((2 * NZ,)), S((NE,)), S((NE,)),
        S((NZ,)), S((NZ,)), S((1,)), S((1,)), S((NE,)), S((NE,)),
        S((2, far)), S((2, far)), S((2, far)), S((2, far)), S((2, NZ)), S((2, NZ)),
        S((2,)), S((2,)), S((2, far)), S((2, far)), S((2, far)), S((2, far)),
        S((NE,)), S((NE,)), S((NZ,)), S((NZ,)), S((NZ,)), S((NZ,)),
    ]
    in_specs = [hbm] + [vmem] * 12 + [hbm] + [vmem] * 3 + [hbm] * 3
    call = pl.pallas_call(
        functools.partial(kernel, (NE, NZ, ROWS, MC, CAP)),
        out_shape=(
            jax.ShapeDtypeStruct((ROWS, NS, WB), BF16),
            jax.ShapeDtypeStruct((3, ROWS, WB), BF16),
            jax.ShapeDtypeStruct((NE * ROWS, WB), BF16),
        ),
        in_specs=in_specs,
        out_specs=(hbm, hbm, vmem),
        scratch_shapes=scratch,
        compiler_params=pltpu.CompilerParams(
            collective_id=0, has_side_effects=True, vmem_limit_bytes=56 * 1024 * 1024
        ),
        name="decode_step",
    )
    ssm_new, conv_new, layer = call(
        ssm_state, conv_state.transpose(1, 0, 2), new_slot.reshape(NZ, LW), conv_input, gate_input,
        conv_weight, conv_bias.reshape(1, WB), x_proj_weight.T, step_weight, step_bias.reshape(1, WB),
        decay_log, skip_gain.reshape(1, WB), out_proj_weight, residual, norm_gain.reshape(2 * NE, LANES),
        routes.T, gate_weight.T, expert_gate[0].T, expert_up[0].T, expert_down[0],
    )
    return ssm_new, conv_new.transpose(1, 0, 2), layer


def solution(mesh):
    in_specs = (
        P("expert", None, "dp"), P("expert", None, "dp"), P(), P("expert", "dp"), P("expert", "dp"),
        P(None, "dp"), P("dp"), P("dp", None), P(None, "dp"), P("dp"), P(None, "dp"), P("dp"),
        P("dp", "expert"), P(None, "expert"), P(), P(), P(),
        P("expert", None, "dp"), P("expert", None, "dp"), P("expert", "dp", None),
    )
    out_specs = (P("expert", None, "dp"), P("expert", None, "dp"), P(None, "expert"))
    return jax.shard_map(body, mesh=mesh, in_specs=in_specs, out_specs=out_specs, check_vma=False)
```

time: 588 us -> 134 us (0.23)
  the two profiles are of different devices: /device:TPU:97 before, /device:TPU:1 now
where the time goes in v1:
time: 134 us
  Pallas kernels  128 us (96%)
  local copies, waits for them, and re-layouts  5.27 us (4%)
    pallas_call x1, Pallas kernels, body(): call(ssm_state, conv_state.transpose(1, 0, 2), new_slot.reshape(NZ, LW),...  128 us
    unnamed x3, local copies, waits for them, and re-layouts  5.27 us

profile of v1, /device:TPU:1, one launch (start us, length us, event | category | flops | bytes accessed | tf_op | source)
XLA Modules:
  0.0 133.7 jit_solution(9634825416547246794)
XLA Ops:
  0.6 127.8 %decode_step.1 = (bf16[64,16,256]{2,1,0:T(8,128)(2,1)}, bf16[3,64,256]{2,1,0:T(8,128)(2,1)}, bf16[1024,256]{1,0:T(8,128)(2,1)}) custom-call(bf16[64,16,256]{2,1,0:T(8,128)(2,1)} %ssm_hbm.1, bf16[3,64,256]{2,1,0:T(8,128)(2,1)} %bitcast.21, s32[8,128]{1,0:T(8,128)} %bitcast.26, bf16[64,256]{1,0:T(8,128)(2,1)} %cin_ref.1, bf16[64,256]{1,0:T(8,128)(2,1)} %gin_ref.1, ...), custom_call_target="tpu_custom_call" | custom-call | tf_op jit(solution)/shard_map/decode_step/pallas_call | solution.py:565
  128.4 1.9 %copy.26 = bf16[64,16,256]{2,1,0:T(8,128)(2,1)} copy(bf16[64,16,256]{2,1,0:T(8,128)(2,1)} %get-tuple-element.12) | data formatting | bytes 1048576
  130.3 1.5 %copy.27 = bf16[64,3,256]{2,0,1:T(8,128)(2,1)} copy(bf16[64,3,256]{2,0,1:T(8,128)(2,1)} %bitcast.22) | data formatting | bytes 196608
  131.8 1.9 %copy.28 = bf16[1024,256]{1,0:T(8,128)(2,1)} copy(bf16[1024,256]{1,0:T(8,128)(2,1)} %get-tuple-element.14) | data formatting | bytes 1048576

commit v2 on v1

v2 whole, which is shorter than its diff:
```python
import functools

import jax
import jax.numpy as jnp
from jax import lax
from jax.experimental import pallas as pl
from jax.experimental.pallas import tpu as pltpu
from jax.sharding import PartitionSpec as P

MESH = pl.DeviceIdType.MESH
F32 = jnp.float32
BF16 = jnp.bfloat16
LANES = 128


def iota(shape, axis):
    return lax.broadcasted_iota(jnp.int32, shape, axis)


def ones_where(mask):
    return jnp.where(mask, 1.0, 0.0)


def dot(a, b):
    return jnp.dot(a, b, preferred_element_type=F32)


def dot_t(a, b):
    return lax.dot_general(a, b, (((1,), (1,)), ((), ())), preferred_element_type=F32)


def silu(v):
    return v / (1.0 + jnp.exp(-v))


def times(lo, hi, step):
    def run(i, carry):
        step(i)
        return carry

    lax.fori_loop(lo, hi, run, 0)


def kernel(
    dims,
    ssm_hbm, conv_hbm, slot_hbm, cin_hbm, gin_hbm, cw_hbm, cb_hbm, xp_hbm, sw_hbm, sb_hbm,
    dl_hbm, sg_hbm, wo_hbm, res_hbm, ng_hbm, rt_hbm, gw_hbm, wg_hbm, wu_hbm, wd_hbm,
    ssm_out, conv_out, layer_out,
    conv_ref, slot_ref, cin_ref, gin_ref, cw_ref, cb_ref, xp_ref, sw_ref, sb_ref,
    dl_ref, sg_ref, wo_ref, ng_ref, rt_ref, gw_ref,
    ssm_v, ssm_f, moved_v, res_v, wg_v, wu_v, wd_v,
    conv_s, conv_r, ssm_s, ssm_r, ssm_o, conv_o,
    proj_s, proj_r, proj_c, proj_g,
    gat, mix_s, mix_b, mix_t, mix_r, stream_v,
    disp_s, xb, xn, acc_g, acc_u, hid, yp, ysib, yrs, yrr, yls, ylr,
    ret_s, ret_r, disp_v, dhi_v, dlo_v, outg,
    load_sem, cs_sem, cr_sem, ss_sem, sr_sem, store_sem,
    ps_sem, pr_sem, qs_sem, qr_sem, gs_sem, gr_sem,
    ms_sem, mr_sem, bs_sem, br_sem, ds_sem, dr_sem,
    xrs, xrr, xls, xlr, xss, xsr,
    yss_sem, ysr_sem, yrs_sem, yrr_sem, yls_sem, ylr_sem,
    rs_sem, rr_sem, os_sem, or_sem, ts_sem, tr_sem, out_sem,
):
    NE, NZ, ROWS, MC, CAP = dims
    ND = 2 * NZ
    PC = 2 * CAP
    LW = 2 * ROWS
    NS = dl_ref.shape[0]
    WB = cin_ref.shape[1]
    RK = sw_ref.shape[0]
    D = NE * WB
    NP = yrs.shape[0]
    HE = NE // NP
    MP = xn.shape[1]
    shift = ROWS.bit_length() - 1
    d = lax.axis_index("dp")
    e = lax.axis_index("expert")
    z = d // 2
    c = d % 2

    def remote(src, dst, ssem, rsem, dev):
        return pltpu.make_async_remote_copy(
            src_ref=src, dst_ref=dst, send_sem=ssem, recv_sem=rsem, device_id=dev, device_id_type=MESH
        )

    ending = []

    def go(copy):
        copy.start()
        ending.append(copy.wait_send)

    barrier = pltpu.get_barrier_semaphore()
    times(1, NE, lambda i: pl.semaphore_signal(barrier, inc=1, device_id=(d, (e + i) % NE), device_id_type=MESH))
    times(1, ND, lambda i: pl.semaphore_signal(barrier, inc=1, device_id=((d + i) % ND, e), device_id_type=MESH))

    row0 = pl.multiple_of(z * LW, LW)
    lane0 = pl.multiple_of(c * LANES, LANES)
    pair = pl.ds(row0, LW)
    sources = [
        (conv_hbm, conv_ref), (slot_hbm, slot_ref), (ssm_hbm, ssm_v), (rt_hbm.at[:, pair], rt_ref),
        (gw_hbm.at[:, pair], gw_ref), (cin_hbm, cin_ref), (cw_hbm, cw_ref), (cb_hbm, cb_ref), (xp_hbm, xp_ref),
        (sw_hbm, sw_ref), (sb_hbm, sb_ref), (dl_hbm, dl_ref), (sg_hbm, sg_ref), (gin_hbm, gin_ref), (wo_hbm, wo_ref),
        (res_hbm.at[pair, pl.ds(lane0, LANES)], res_v), (ng_hbm, ng_ref), (wg_hbm, wg_v), (wu_hbm, wu_v), (wd_hbm, wd_v),
    ]
    loads = [pltpu.make_async_copy(src, dst, load_sem.at[i]) for i, (src, dst) in enumerate(sources)]
    for load in loads:
        load.start()

    def loaded(lo, hi):
        for load in loads[lo:hi]:
            load.wait()

    loaded(0, 2)

    mine = slot_ref[pl.ds(e // 2, 1), :]
    mine = jnp.where(e % 2 == 0, mine[:, :ROWS], mine[:, ROWS:])
    target = lax.shift_right_logical(mine, shift)
    target_hot = ones_where(iota((NE, ROWS), 0) == target)
    before = ones_where(iota((ROWS, ROWS), 0) < iota((ROWS, ROWS), 1)).astype(BF16)
    ahead = dot(target_hot.astype(BF16), before)
    earlier = jnp.sum(target_hot * ahead, axis=0, keepdims=True).astype(jnp.int32)
    pack = ones_where(iota((NE * MC, ROWS), 0) == target * MC + earlier).astype(BF16)
    for k in range(3):
        conv_s[:, k] = dot(pack, conv_ref[k]).reshape(NE, MC, WB).astype(BF16)

    loaded(2, 3)
    ssm_f[...] = ssm_v[...].astype(F32)
    for n in range(NS):
        ssm_s[:, n] = dot(pack, ssm_f[:, n, :].astype(BF16)).reshape(NE, MC, WB).astype(BF16)

    slots = slot_ref[...]
    arriving = ones_where(lax.shift_right_logical(slots, shift) == e)
    lane = iota((LW, LW), 1)
    sub = iota((LW, LW), 0)
    before2 = ones_where((sub < lane) & ((sub < ROWS) == (lane < ROWS))).astype(BF16)
    rank = dot(arriving.astype(BF16), before2)
    place = (slots & (ROWS - 1)).astype(F32) + 1.0
    half = iota((NZ, LW), 1) >= ROWS
    to_lane = iota((NZ, NE * MC), 1) - iota((NZ, NE * MC), 0) * (2 * MC)
    spread = jnp.zeros((NZ, NE * MC), F32)
    for h in range(2):
        live = (arriving > 0.0) & (half == bool(h))
        for k in range(MC):
            found = jnp.sum(jnp.where(live & (rank == float(k)), place, 0.0), axis=1, keepdims=True)
            spread = spread + jnp.where(to_lane == h * MC + k, found, 0.0)
    row_of = jnp.sum(spread, axis=0, keepdims=True).astype(jnp.int32) - 1
    unpack = ones_where(iota((ROWS, NE * MC), 0) == row_of).astype(BF16)

    loaded(3, 5)
    r0 = rt_ref[0:1, :]
    r1 = rt_ref[1:2, :]
    g0 = gw_ref[0:1, :]
    g1 = gw_ref[1:2, :]
    expert_id = iota((NE, LW), 0)
    named = ones_where((expert_id == r0) | (expert_id == r1))
    weight = jnp.where(expert_id == r0, g0, 0.0) + jnp.where(expert_id == r1, g1, 0.0)
    w_hi = weight.astype(BF16).astype(F32)
    w_lo = weight - w_hi
    in_block = dot(named.astype(BF16), before2).astype(jnp.int32)
    seat = in_block + jnp.where(iota((NE, LW), 1) >= ROWS, CAP, 0)
    seat = jnp.where(named > 0.0, seat, -1)
    seat_id = iota((PC, LW), 0)
    rows_d, rows_hi, rows_lo = [], [], []
    for k in range(NE):
        hit = seat_id == seat[k : k + 1, :]
        rows_d.append(jnp.where(hit, 1.0, 0.0))
        rows_hi.append(jnp.where(hit, w_hi[k : k + 1, :], 0.0))
        rows_lo.append(jnp.where(hit, w_lo[k : k + 1, :], 0.0))
    disp_v[...] = jnp.concatenate(rows_d, axis=0).astype(BF16)
    dhi_v[...] = jnp.concatenate(rows_hi, axis=0).T.astype(BF16)
    dlo_v[...] = jnp.concatenate(rows_lo, axis=0).T.astype(BF16)

    def all_sent(some, ssem, rsem):
        ending.append(remote(some, some, ssem.at[0], rsem.at[0], (d, e)).wait_send)

    def all_received(some, ssem, rsem):
        remote(some, some, ssem.at[0], rsem.at[0], (d, e)).wait_recv()

    def to_experts(src_of, dst, some, ssem, rsem):
        for i in range(1, NE):
            p = (e + i) % NE
            remote(src_of(p), dst, ssem.at[0], rsem.at[0], (d, p)).start()
        all_sent(some, ssem, rsem)

    pl.semaphore_wait(barrier, NE - 1 + ND - 1)

    to_experts(lambda p: conv_s.at[p], conv_r.at[e], conv_s.at[pl.ds(0, NE - 1)], cs_sem, cr_sem)
    conv_r[e] = conv_s[e]
    ssm_r[e] = ssm_s[e]

    loaded(5, 9)
    all_received(conv_r.at[pl.ds(0, NE - 1)], cs_sem, cr_sem)
    to_experts(lambda p: ssm_s.at[p], ssm_r.at[e], ssm_s.at[pl.ds(0, NE - 1)], ss_sem, sr_sem)
    window = []
    for k in range(3):
        got = conv_r[:, k].astype(F32).reshape(NE * MC, WB).astype(BF16)
        window.append(dot(unpack, got))
    conv_o[0] = window[1].astype(BF16)
    conv_o[1] = window[2].astype(BF16)
    conv_o[2] = cin_ref[...]
    window.append(cin_ref[...].astype(F32))
    total = window[0] * cw_ref[0:1, :]
    for k in range(1, 4):
        total = total + window[k] * cw_ref[k : k + 1, :]
    activated = silu(total + cb_ref[...]).astype(BF16)
    act = activated.astype(F32)
    partial = dot_t(activated, xp_ref[...])
    RZ = ROWS // NZ
    proj_s[...] = jnp.zeros_like(proj_s)
    proj_s[:, :, : RK + 2 * NS] = partial.reshape(NZ, RZ, RK + 2 * NS)

    def proj_src(p):
        return proj_s.at[p // 2, :, pl.ds(pl.multiple_of((p % 2) * LANES, LANES), RK)]

    def to_dp(src_of, dst, some, ssem, rsem):
        for i in range(1, ND):
            p = (d + i) % ND
            remote(src_of(p), dst, ssem.at[0], rsem.at[0], (p, e)).start()
        all_sent(some, ssem, rsem)

    others = pl.ds(0, ND - 1)
    to_dp(proj_src, proj_r.at[d], proj_r.at[others], ps_sem, pr_sem)
    proj_r[d] = proj_s[z, :, pl.ds(lane0, RK)]
    store_conv = pltpu.make_async_copy(conv_o, conv_out, store_sem.at[0])
    store_conv.start()
    ending.append(store_conv.wait)

    all_received(proj_r.at[others], ps_sem, pr_sem)
    summed = proj_r[0]
    for k in range(1, ND):
        summed = summed + proj_r[k]
    proj_c[...] = summed
    to_dp(lambda p: proj_c, proj_g.at[c, z], proj_r.at[others], qs_sem, qr_sem)
    proj_g[c, z] = summed
    all_received(ssm_r.at[pl.ds(0, NE - 1)], ss_sem, sr_sem)
    for n in range(NS):
        got = ssm_r[:, n].astype(F32).reshape(NE * MC, WB).astype(BF16)
        moved_v[n] = dot(unpack, got)
    loaded(9, 14)
    gate = silu(gin_ref[...].astype(F32))
    decay = -jnp.exp(dl_ref[...])
    all_received(proj_r.at[others], qs_sem, qr_sem)
    step_low = proj_g[0].reshape(ROWS, RK)
    coef = proj_g[1][:, :, RK - LANES :].reshape(ROWS, LANES)
    mean = jnp.sum(step_low * step_low, axis=1, keepdims=True) * (1.0 / RK)
    step_norm = (step_low * lax.rsqrt(mean + 1e-06)).astype(BF16)
    pre = dot(step_norm, sw_ref[...]) + sb_ref[...]
    step = jnp.maximum(pre, 0.0) + jnp.log1p(jnp.exp(-jnp.abs(pre)))
    push = step * act

    y = sg_ref[...] * act
    read = jnp.zeros_like(y)
    for n in range(NS):
        state = jnp.exp(step * decay[n : n + 1, :]) * moved_v[n] + push * coef[:, n : n + 1]
        ssm_f[:, n, :] = state
        read = read + coef[:, NS + n : NS + n + 1] * state
    gated = ((read + y) * gate).astype(BF16)
    gat[e] = gated
    for i in range(1, NE):
        remote(gat.at[e], gat.at[e], gs_sem.at[0], gr_sem.at[e], (d, (e + i) % NE)).start()
    all_sent(gat.at[pl.ds(0, NE - 1)], gs_sem, gr_sem)
    ssm_o[...] = ssm_f[...].astype(BF16)
    store_ssm = pltpu.make_async_copy(ssm_o, ssm_out, store_sem.at[1])
    store_ssm.start()
    ending.append(store_ssm.wait)

    loaded(14, 16)
    sibling = (2 * z + 1 - c, e)

    def swap_mix(p):
        return remote(mix_s.at[1 - c, p], mix_b.at[p], bs_sem.at[0], br_sem.at[p], sibling)

    def arrived(p):
        @pl.when(p != e)
        def _():
            remote(gat.at[p], gat.at[p], gs_sem.at[0], gr_sem.at[p], (d, p)).wait_recv()

    def project(p):
        arrived(2 * p)
        arrived(2 * p + 1)
        mixed = dot(gat[pl.ds(2 * p, 2)].reshape(LW, WB), wo_ref[...])
        mix_s[0, p] = mixed[:, :LANES].astype(BF16)
        mix_s[1, p] = mixed[:, LANES:].astype(BF16)
        swap_mix(p).start()

    def send_mix(i):
        p = (z + i) % NZ
        return remote(mix_t.at[p], mix_r.at[z], ms_sem.at[0], mr_sem.at[0], (2 * p + c, e))

    def join(i):
        p = (z + i) % NZ
        swap_mix(p).wait_recv()
        mix_t[p] = (mix_s[c, p].astype(F32) + mix_b[p].astype(F32)).astype(BF16)
        if i > 0:
            send_mix(i).start()

    all_sent(mix_b, bs_sem, br_sem)
    order = [*range(1, NZ), 0]
    for at, i in enumerate(order):
        project((z + i) % NZ)
        if at > 0:
            join(order[at - 1])
    join(0)
    mix_r[z] = mix_t[z]
    all_sent(mix_t.at[pl.ds(0, NZ - 1)], ms_sem, mr_sem)

    all_received(mix_r.at[pl.ds(0, NZ - 1)], ms_sem, mr_sem)
    mixed = mix_r[0].astype(F32)
    for k in range(1, NZ):
        mixed = mixed + mix_r[k].astype(F32)
    stream = (res_v[...].astype(F32) + mixed).astype(BF16)
    stream_v[...] = stream

    disp_s[...] = dot(disp_v[...], stream).reshape(NE, PC, LANES).astype(BF16)
    to_experts(lambda p: disp_s.at[p], xb.at[c, z, e], disp_s.at[pl.ds(0, NE - 1)], ds_sem, dr_sem)
    xb[c, z, e] = disp_s[e]
    all_received(disp_s.at[pl.ds(0, NE - 1)], ds_sem, dr_sem)

    right = (2 * ((z + 1) % NZ) + c, e)
    left = (2 * ((z + NZ - 1) % NZ) + c, e)
    far = NZ // 2
    pieces = range(NP)
    hops_r = [far if h < NP // 2 else NZ - 1 - far for h in pieces]
    hops_l = [NZ - 1 - far if h < NP // 2 else far for h in pieces]
    halves = [pl.ds(h * HE, HE) for h in pieces]

    def back(s):
        return (z + NZ - s) % NZ

    def ahead_z(s):
        return (z + s) % NZ

    def ring_right(h, s):
        p = back(s)
        part = xb.at[c, p, halves[h]]
        return remote(part, part, xrs.at[h, s], xrr.at[h, s], right)

    def ring_left(h, s):
        p = ahead_z(s)
        part = xb.at[c, p, halves[h]]
        return remote(part, part, xls.at[h, s], xlr.at[h, s], left)

    def wait_right(h, s):
        part = xb.at[c, back(s + 1), halves[h]]
        remote(part, part, xrs.at[h, s], xrr.at[h, s], right).wait_recv()

    def wait_left(h, s):
        part = xb.at[c, ahead_z(s + 1), halves[h]]
        remote(part, part, xls.at[h, s], xlr.at[h, s], left).wait_recv()

    def over(p):
        return remote(xb.at[c, p], xb.at[c, p], xss.at[0], xsr.at[p], sibling)

    def wait_over(p):
        remote(xb.at[1 - c, p], xb.at[1 - c, p], xss.at[0], xsr.at[p], sibling).wait_recv()

    all_sent(xb.at[0], xss, xsr)

    def normalise(o, p):
        square = jnp.zeros((PC, LANES), F32)
        for k in range(NE):
            for m in range(2):
                v = xb[m, p, k].astype(F32)
                square = square + v * v
        scale = lax.rsqrt(jnp.sum(square, axis=1, keepdims=True) * (1.0 / D) + 1e-05)
        for k in range(NE):
            for m in range(2):
                v = xb[m, p, k].astype(F32) * scale * ng_ref[2 * k + m : 2 * k + m + 1, :]
                if MP > PC:
                    v = jnp.concatenate([v, jnp.zeros((MP - PC, LANES), F32)], axis=0)
                xn[o, :, (2 * k + m) * LANES : (2 * k + m + 1) * LANES] = v.astype(BF16)

    steps = [[(0, z, 0)]]
    for s in range(1, far):
        steps.append([(2 * s - 1, back(s), -s), (2 * s, ahead_z(s), s)])
    steps.append([(NZ - 1, ahead_z(far), far)])
    number = {off % NZ: o for group in steps for o, _, off in group}
    FIRST = sum(len(group) for group in steps[: max(1, far - 1)])
    KC = min(D, 1024)

    def gate_up(lo, hi):
        rows = pl.ds(lo * MP, (hi - lo) * MP)
        acc_g[rows] = jnp.zeros(((hi - lo) * MP, acc_g.shape[1]), F32)
        acc_u[rows] = jnp.zeros(((hi - lo) * MP, acc_u.shape[1]), F32)

        def depth(k):
            at = pl.ds(pl.multiple_of(k * KC, KC), KC)
            x = xn[lo:hi, :, at].reshape((hi - lo) * MP, KC)
            acc_g[rows] += dot_t(x, wg_v[:, at])
            acc_u[rows] += dot_t(x, wu_v[:, at])

        times(0, D // KC, depth)
        hid[rows] = (silu(acc_g[rows]) * acc_u[rows]).astype(BF16)

    def settle(group):
        for o, p, _ in group:
            wait_over(p)
            normalise(o, p)

    loaded(16, 19)
    for s in range(far + 1):
        for h in pieces:
            if 0 < s <= hops_r[h]:
                wait_right(h, s - 1)
            if s < hops_r[h]:
                go(ring_right(h, s))
            if 0 < s <= hops_l[h]:
                wait_left(h, s - 1)
            if s < hops_l[h]:
                go(ring_left(h, s))
        for _, p, _ in steps[s]:
            over(p).start()
        if s > 0:
            settle(steps[s - 1])
        if s == max(1, far - 1):
            gate_up(0, FIRST)
    settle(steps[far])
    gate_up(FIRST, NZ)
    loaded(19, 20)

    def down(lo, hi):
        def one(k):
            at = pl.ds(pl.multiple_of(k * WB, WB), WB)
            out = dot(hid[lo * MP : hi * MP], wd_v[:, at]).reshape(hi - lo, MP, WB)[:, :PC].astype(BF16)
            yp[0, lo:hi, k] = out[:, :, :LANES]
            yp[1, lo:hi, k] = out[:, :, LANES:]

        times(0, NE, one)

    def swap_y(g):
        lo, hi = ((FIRST, NZ), (0, FIRST))[g]
        part = pl.ds(lo, hi - lo)
        return remote(yp.at[1 - c, part], ysib.at[part], yss_sem.at[g], ysr_sem.at[g], sibling)

    down(FIRST, NZ)
    go(swap_y(0))

    def own(h, off):
        o = number[off % NZ]
        return yp[c, o, h * HE : (h + 1) * HE].astype(F32) + ysib[o, h * HE : (h + 1) * HE].astype(F32)

    def chain_right(h, s):
        return remote(yrs.at[h, s], yrr.at[h, s], yrs_sem.at[h, s], yrr_sem.at[h, s], right)

    def chain_left(h, s):
        return remote(yls.at[h, s], ylr.at[h, s], yls_sem.at[h, s], ylr_sem.at[h, s], left)

    def chain_step(h, s):
        if s < hops_r[h]:
            part = own(h, hops_r[h] - s)
            if s > 0:
                chain_right(h, s - 1).wait_recv()
                part = part + yrr[h, s - 1].astype(F32)
            yrs[h, s] = part.astype(BF16)
            go(chain_right(h, s))
        if s < hops_l[h]:
            part = own(h, s - hops_l[h])
            if s > 0:
                chain_left(h, s - 1).wait_recv()
                part = part + ylr[h, s - 1].astype(F32)
            yls[h, s] = part.astype(BF16)
            go(chain_left(h, s))

    swap_y(0).wait_recv()
    if FIRST <= NZ - 3:
        for h in pieces:
            chain_step(h, 0)
        down(0, FIRST)
        go(swap_y(1))
        swap_y(1).wait_recv()
    else:
        down(0, FIRST)
        go(swap_y(1))
        swap_y(1).wait_recv()
        for h in pieces:
            chain_step(h, 0)
    for s in range(1, far):
        for h in pieces:
            chain_step(h, s)
    def returned(k):
        return remote(ret_s.at[k], ret_r.at[e], rs_sem.at[0], rr_sem.at[0], (d, k))

    def give_back(k):
        @pl.when(e != k)
        def _():
            returned(k).start()

        @pl.when(e == k)
        def _():
            ret_r[k] = ret_s[k]

    all_sent(ret_s.at[pl.ds(0, NE - 1)], rs_sem, rr_sem)
    for h in pieces:
        part = own(h, 0)
        if hops_r[h] > 0:
            chain_right(h, hops_r[h] - 1).wait_recv()
            part = part + yrr[h, hops_r[h] - 1].astype(F32)
        if hops_l[h] > 0:
            chain_left(h, hops_l[h] - 1).wait_recv()
            part = part + ylr[h, hops_l[h] - 1].astype(F32)
        ret_s[h * HE : (h + 1) * HE] = part.astype(BF16)
        for k in range(h * HE, (h + 1) * HE):
            give_back(k)

    all_received(ret_r.at[pl.ds(0, NE - 1)], rs_sem, rr_sem)
    back_rows = ret_r[...].astype(F32).reshape(NE * PC, LANES).astype(BF16)
    final = stream_v[...].astype(F32) + dot(dhi_v[...], back_rows) + dot(dlo_v[...], back_rows)
    outg[c, z] = final.astype(BF16)

    def send_out(i):
        p = (z + i) % NZ
        return remote(outg.at[c, z], outg.at[c, z], os_sem.at[0], or_sem.at[z], (2 * p + c, e))

    def wait_out(i):
        p = (z + NZ - i) % NZ
        remote(outg.at[c, p], outg.at[c, p], os_sem.at[i], or_sem.at[p], (2 * p + c, e)).wait_recv()

    def pass_out(p):
        return remote(outg.at[c, p], outg.at[c, p], ts_sem.at[0], tr_sem.at[p], sibling)

    times(1, NZ, lambda i: send_out(i).start())
    all_sent(outg.at[0, pl.ds(0, NZ - 1)], os_sem, or_sem)
    pass_out(z).start()
    all_sent(outg.at[0], ts_sem, tr_sem)

    def relay(i):
        wait_out(i)
        pass_out((z + NZ - i) % NZ).start()

    times(1, NZ, relay)

    def store_out(m, p):
        at = layer_out.at[pl.ds(pl.multiple_of(p * LW, LW), LW), pl.ds(pl.multiple_of(m * LANES, LANES), LANES)]
        return pltpu.make_async_copy(outg.at[m, p], at, out_sem.at[m, p])

    def wait_pass(i):
        p = (z + NZ - i) % NZ
        remote(outg.at[1 - c, p], outg.at[1 - c, p], ts_sem.at[p], tr_sem.at[p], sibling).wait_recv()
        store_out(c, p).start()
        store_out(1 - c, p).start()

    times(0, NZ, wait_pass)

    def stored(p):
        store_out(c, p).wait()
        store_out(1 - c, p).wait()

    times(0, NZ, stored)

    for wait in ending:
        wait()


def hand_over(a, b, c, oa, ob, oc, va, vb, vc, sem):
    through = ((a, va, oa), (b, vb, ob), (c, vc, oc))
    first = [pltpu.make_async_copy(x, v, sem.at[i]) for i, (x, v, _) in enumerate(through)]
    second = [pltpu.make_async_copy(v, y, sem.at[i]) for i, (_, v, y) in enumerate(through)]
    for copy in first:
        copy.start()
    for one, two in zip(first, second):
        one.wait()
        two.start()
    for copy in second:
        copy.wait()


def body(
    ssm_state, conv_state, new_slot, conv_input, gate_input, conv_weight, conv_bias, x_proj_weight,
    step_weight, step_bias, decay_log, skip_gain, out_proj_weight, residual, norm_gain, routes,
    gate_weight, expert_gate, expert_up, expert_down,
):
    ROWS, NS, WB = ssm_state.shape
    NE = lax.axis_size("expert")
    NZ = lax.axis_size("dp") // 2
    RK = step_weight.shape[0]
    FB = expert_gate.shape[2]
    MC = 2 * ROWS // NE
    CAP = min(ROWS, 5 * ROWS * routes.shape[1] // (2 * NE))
    PC, LW, D, NP = 2 * CAP, 2 * ROWS, NE * WB, 4
    HE = NE // NP
    MP = (PC + 15) // 16 * 16
    RZ = ROWS // NZ
    far = NZ // 2
    hbm = pl.BlockSpec(memory_space=pl.ANY)
    V, S = pltpu.VMEM, pltpu.SemaphoreType.DMA
    scratch = [
        V((3, ROWS, WB), BF16), V((NZ, LW), jnp.int32), V((ROWS, WB), BF16), V((ROWS, WB), BF16),
        V((4, WB), F32), V((1, WB), F32), V((RK + 2 * NS, WB), BF16), V((RK, WB), BF16), V((1, WB), F32),
        V((NS, WB), F32), V((1, WB), F32), V((WB, WB), BF16), V((2 * NE, LANES), F32),
        V((2, LW), jnp.int32), V((2, LW), F32),
        V((ROWS, NS, WB), BF16), V((ROWS, NS, WB), F32), V((NS, ROWS, WB), F32), V((LW, LANES), BF16),
        V((FB, D), BF16), V((FB, D), BF16), V((FB, D), BF16),
        V((NE, 3, MC, WB), BF16), V((NE, 3, MC, WB), BF16),
        V((NE, NS, MC, WB), BF16), V((NE, NS, MC, WB), BF16),
        V((ROWS, NS, WB), BF16), V((3, ROWS, WB), BF16),
        V((NZ, RZ, RK + LANES), F32), V((2 * NZ, RZ, RK), F32), V((RZ, RK), F32), V((2, NZ, RZ, RK), F32),
        V((NE, ROWS, WB), BF16), V((2, NZ, LW, LANES), BF16), V((NZ, LW, LANES), BF16),
        V((NZ, LW, LANES), BF16), V((NZ, LW, LANES), BF16), V((LW, LANES), BF16),
        V((NE, PC, LANES), BF16), V((2, NZ, NE, PC, LANES), BF16), V((NZ, MP, D), BF16),
        V((NZ * MP, FB), F32), V((NZ * MP, FB), F32), V((NZ * MP, FB), BF16),
        V((2, NZ, NE, PC, LANES), BF16), V((NZ, NE, PC, LANES), BF16),
        V((NP, far, HE, PC, LANES), BF16), V((NP, far, HE, PC, LANES), BF16),
        V((NP, far, HE, PC, LANES), BF16), V((NP, far, HE, PC, LANES), BF16),
        V((NE, PC, LANES), BF16), V((NE, PC, LANES), BF16),
        V((NE * PC, LW), BF16), V((LW, NE * PC), BF16), V((LW, NE * PC), BF16), V((2, NZ, LW, LANES), BF16),
        S((20,)), S((NE,)), S((NE,)), S((NE,)), S((NE,)), S((2,)),
        S((2 * NZ,)), S((2 * NZ,)), S((2 * NZ,)), S((2 * NZ,)), S((NE,)), S((NE,)),
        S((NZ,)), S((NZ,)), S((NZ,)), S((NZ,)), S((NE,)), S((NE,)),
        S((NP, far)), S((NP, far)), S((NP, far)), S((NP, far)), S((NZ,)), S((NZ,)),
        S((2,)), S((2,)), S((NP, far)), S((NP, far)), S((NP, far)), S((NP, far)),
        S((NE,)), S((NE,)), S((NZ,)), S((NZ,)), S((NZ,)), S((NZ,)), S((2, NZ)),
    ]
    call = pl.pallas_call(
        functools.partial(kernel, (NE, NZ, ROWS, MC, CAP)),
        out_shape=(
            jax.ShapeDtypeStruct((ROWS, NS, WB), BF16),
            jax.ShapeDtypeStruct((3, ROWS, WB), BF16),
            jax.ShapeDtypeStruct((NE * ROWS, WB), BF16),
        ),
        in_specs=[hbm] * 20,
        out_specs=(hbm, hbm, hbm),
        scratch_shapes=scratch,
        compiler_params=pltpu.CompilerParams(
            collective_id=0, has_side_effects=True, vmem_limit_bytes=56 * 1024 * 1024
        ),
        name="decode_step",
    )
    ssm_new, conv_new, layer = call(
        ssm_state, conv_state.transpose(1, 0, 2), new_slot.reshape(NZ, LW), conv_input, gate_input,
        conv_weight, conv_bias.reshape(1, WB), x_proj_weight.T, step_weight, step_bias.reshape(1, WB),
        decay_log, skip_gain.reshape(1, WB), out_proj_weight, residual, norm_gain.reshape(2 * NE, LANES),
        routes.T, gate_weight.T, expert_gate[0].T, expert_up[0].T, expert_down[0],
    )
    shapes = [jax.ShapeDtypeStruct(v.shape, v.dtype) for v in (ssm_new, conv_new, layer)]
    ssm_new, conv_new, layer = pl.pallas_call(
        hand_over, out_shape=shapes, in_specs=[hbm] * 3, out_specs=[hbm] * 3, scratch_shapes=[*(V(v.shape, v.dtype) for v in shapes), S((3,))], name="hand_over"
    )(ssm_new, conv_new, layer)
    return ssm_new, conv_new.transpose(1, 0, 2), layer


def solution(mesh):
    in_specs = (
        P("expert", None, "dp"), P("expert", None, "dp"), P(), P("expert", "dp"), P("expert", "dp"),
        P(None, "dp"), P("dp"), P("dp", None), P(None, "dp"), P("dp"), P(None, "dp"), P("dp"),
        P("dp", "expert"), P(None, "expert"), P(), P(), P(),
        P("expert", None, "dp"), P("expert", None, "dp"), P("expert", "dp", None),
    )
    out_specs = (P("expert", None, "dp"), P("expert", None, "dp"), P(None, "expert"))
    return jax.shard_map(body, mesh=mesh, in_specs=in_specs, out_specs=out_specs, check_vma=False)
```

time: 134 us -> 121 us (0.903)
  Pallas kernels: 128 us -> 121 us
  local copies, waits for them, and re-layouts: 5.27 us -> 0 us
    pallas_call x1, Pallas kernels: 128 us -> 119 us  [body(): call(ssm_state, conv_state.transpose(1, 0, 2), new_slot.reshape(NZ, LW),...]
    unnamed x3 -> x0, local copies, waits for them, and re-layouts: 5.27 us -> none
    pallas_call x0 -> x1, Pallas kernels: none -> 2.07 us  [body(): pl.pallas_call(hand_over, out_shape=shapes, in_specs=[hbm] * 3, out_specs...]
where the time goes in v2:
time: 121 us
  Pallas kernels  121 us (100%)
    pallas_call x1, Pallas kernels, body(): call(ssm_state, conv_state.transpose(1, 0, 2), new_slot.reshape(NZ, LW),...  119 us

profile of v2, /device:TPU:1, one launch (start us, length us, event | category | flops | bytes accessed | tf_op | source)
XLA Modules:
  0.0 121.3 jit_solution(3534810748704609567)
XLA Ops:
  0.6 118.6 %decode_step.1 = (bf16[64,16,256]{2,1,0:T(8,128)(2,1)}, bf16[3,64,256]{2,1,0:T(8,128)(2,1)}, bf16[1024,256]{1,0:T(8,128)(2,1)}) custom-call(bf16[64,16,256]{2,1,0:T(8,128)(2,1)} %ssm_hbm.1, bf16[3,64,256]{2,1,0:T(8,128)(2,1)} %bitcast.21, s32[8,128]{1,0:T(8,128)} %bitcast.25, bf16[64,256]{1,0:T(8,128)(2,1)} %cin_hbm.1, bf16[64,256]{1,0:T(8,128)(2,1)} %gin_hbm.1, ...), custom_call_target="tpu_custom_call" | custom-call | tf_op jit(solution)/shard_map/decode_step/pallas_call | solution.py:628
  119.3 2.1 %hand_over.1 = (bf16[64,16,256]{2,1,0:T(8,128)(2,1)}, bf16[3,64,256]{2,1,0:T(8,128)(2,1)}, bf16[1024,256]{1,0:T(8,128)(2,1)}) custom-call(bf16[64,16,256]{2,1,0:T(8,128)(2,1)} %get-tuple-element.9.a, bf16[3,64,256]{2,1,0:T(8,128)(2,1)} %get-tuple-element.10.b, bf16[1024,256]{1,0:T(8,128)(2,1)} %get-tuple-element.11.c), custom_call_target="tpu_custom_call" | custom-call | tf_op jit(solution)/shard_map/hand_over/pallas_call | solution.py:635

commit v3 on v2

--- a/solution.py
+++ b/solution.py
@@ -57,9 +57,9 @@
     load_sem, cs_sem, cr_sem, ss_sem, sr_sem, store_sem,
     ps_sem, pr_sem, qs_sem, qr_sem, gs_sem, gr_sem,
     ms_sem, mr_sem, bs_sem, br_sem, ds_sem, dr_sem,
-    xrs, xrr, xls, xlr, xss, xsr,
-    yss_sem, ysr_sem, yrs_sem, yrr_sem, yls_sem, ylr_sem,
-    rs_sem, rr_sem, os_sem, or_sem, ts_sem, tr_sem, out_sem,
+    xs_sem, xrr, xlr, xss, xsr,
+    yss_sem, ysr_sem, ys_sem, yrr_sem, ylr_sem,
+    rs_sem, rr_sem, os_sem, or_sem, ts_sem, tr_sem, out_sem, fs_sem, fr_sem,
 ):
     NE, NZ, ROWS, MC, CAP = dims
     ND = 2 * NZ
@@ -85,13 +85,11 @@
 
     ending = []
 
-    def go(copy):
-        copy.start()
-        ending.append(copy.wait_send)
-
     barrier = pltpu.get_barrier_semaphore()
-    times(1, NE, lambda i: pl.semaphore_signal(barrier, inc=1, device_id=(d, (e + i) % NE), device_id_type=MESH))
-    times(1, ND, lambda i: pl.semaphore_signal(barrier, inc=1, device_id=((d + i) % ND, e), device_id_type=MESH))
+    for i in range(1, ND):
+        pl.semaphore_signal(barrier, inc=1, device_id=((d + i) % ND, e), device_id_type=MESH)
+    for i in range(1, NE):
+        pl.semaphore_signal(barrier, inc=1, device_id=(d, (e + i) % NE), device_id_type=MESH)
 
     row0 = pl.multiple_of(z * LW, LW)
     lane0 = pl.multiple_of(c * LANES, LANES)
@@ -333,20 +331,20 @@
     def ring_right(h, s):
         p = back(s)
         part = xb.at[c, p, halves[h]]
-        return remote(part, part, xrs.at[h, s], xrr.at[h, s], right)
+        return remote(part, part, xs_sem.at[0], xrr.at[h, s], right)
 
     def ring_left(h, s):
         p = ahead_z(s)
         part = xb.at[c, p, halves[h]]
-        return remote(part, part, xls.at[h, s], xlr.at[h, s], left)
+        return remote(part, part, xs_sem.at[0], xlr.at[h, s], left)
 
     def wait_right(h, s):
         part = xb.at[c, back(s + 1), halves[h]]
-        remote(part, part, xrs.at[h, s], xrr.at[h, s], right).wait_recv()
+        remote(part, part, xs_sem.at[0], xrr.at[h, s], right).wait_recv()
 
     def wait_left(h, s):
         part = xb.at[c, ahead_z(s + 1), halves[h]]
-        remote(part, part, xls.at[h, s], xlr.at[h, s], left).wait_recv()
+        remote(part, part, xs_sem.at[0], xlr.at[h, s], left).wait_recv()
 
     def over(p):
         return remote(xb.at[c, p], xb.at[c, p], xss.at[0], xsr.at[p], sibling)
@@ -355,6 +353,7 @@
         remote(xb.at[1 - c, p], xb.at[1 - c, p], xss.at[0], xsr.at[p], sibling).wait_recv()
 
     all_sent(xb.at[0], xss, xsr)
+    all_sent(xb.at[0, pl.ds(0, NZ - 1)], xs_sem, xss)
 
     def normalise(o, p):
         square = jnp.zeros((PC, LANES), F32)
@@ -398,22 +397,34 @@
             normalise(o, p)
 
     loaded(16, 19)
+    def ring_step(s, lead):
+        for h in pieces:
+            if (h < NP // 2) == lead:
+                if 0 < s <= hops_r[h]:
+                    wait_right(h, s - 1)
+                if s < hops_r[h]:
+                    ring_right(h, s).start()
+            else:
+                if 0 < s <= hops_l[h]:
+                    wait_left(h, s - 1)
+                if s < hops_l[h]:
+                    ring_left(h, s).start()
+
     for s in range(far + 1):
-        for h in pieces:
-            if 0 < s <= hops_r[h]:
-                wait_right(h, s - 1)
-            if s < hops_r[h]:
-                go(ring_right(h, s))
-            if 0 < s <= hops_l[h]:
-                wait_left(h, s - 1)
-            if s < hops_l[h]:
-                go(ring_left(h, s))
-        for _, p, _ in steps[s]:
-            over(p).start()
+        ring_step(s, True)
+        if s == 0:
+            over(z).start()
+            settle(steps[0])
+        ring_step(s, False)
         if s > 0:
-            settle(steps[s - 1])
+            for _, p, _ in steps[s]:
+                over(p).start()
+        if 0 < s < far - 1:
+            settle(steps[s])
         if s == max(1, far - 1):
             gate_up(0, FIRST)
+    if far > 1:
+        settle(steps[far - 1])
     settle(steps[far])
     gate_up(FIRST, NZ)
     loaded(19, 20)
@@ -430,53 +441,58 @@
     def swap_y(g):
         lo, hi = ((FIRST, NZ), (0, FIRST))[g]
         part = pl.ds(lo, hi - lo)
-        return remote(yp.at[1 - c, part], ysib.at[part], yss_sem.at[g], ysr_sem.at[g], sibling)
+        return remote(yp.at[1 - c, part], ysib.at[part], yss_sem.at[0], ysr_sem.at[g], sibling)
 
     down(FIRST, NZ)
-    go(swap_y(0))
+    swap_y(0).start()
 
     def own(h, off):
         o = number[off % NZ]
         return yp[c, o, h * HE : (h + 1) * HE].astype(F32) + ysib[o, h * HE : (h + 1) * HE].astype(F32)
 
     def chain_right(h, s):
-        return remote(yrs.at[h, s], yrr.at[h, s], yrs_sem.at[h, s], yrr_sem.at[h, s], right)
+        return remote(yrs.at[h, s], yrr.at[h, s], ys_sem.at[0], yrr_sem.at[h, s], right)
 
     def chain_left(h, s):
-        return remote(yls.at[h, s], ylr.at[h, s], yls_sem.at[h, s], ylr_sem.at[h, s], left)
-
-    def chain_step(h, s):
-        if s < hops_r[h]:
-            part = own(h, hops_r[h] - s)
-            if s > 0:
-                chain_right(h, s - 1).wait_recv()
-                part = part + yrr[h, s - 1].astype(F32)
-            yrs[h, s] = part.astype(BF16)
-            go(chain_right(h, s))
-        if s < hops_l[h]:
-            part = own(h, s - hops_l[h])
-            if s > 0:
-                chain_left(h, s - 1).wait_recv()
-                part = part + ylr[h, s - 1].astype(F32)
-            yls[h, s] = part.astype(BF16)
-            go(chain_left(h, s))
+        return remote(yls.at[h, s], ylr.at[h, s], ys_sem.at[0], ylr_sem.at[h, s], left)
+
+    all_sent(ysib, yss_sem, ysr_sem)
+    all_sent(ysib.at[pl.ds(0, NZ - 1)], ys_sem, yss_sem)
+
+    def chain_step(s, lead):
+        for h in pieces:
+            if (h < NP // 2) == lead and s < hops_r[h]:
+                part = own(h, hops_r[h] - s)
+                if s > 0:
+                    chain_right(h, s - 1).wait_recv()
+                    part = part + yrr[h, s - 1].astype(F32)
+                yrs[h, s] = part.astype(BF16)
+                chain_right(h, s).start()
+            if (h < NP // 2) != lead and s < hops_l[h]:
+                part = own(h, s - hops_l[h])
+                if s > 0:
+                    chain_left(h, s - 1).wait_recv()
+                    part = part + ylr[h, s - 1].astype(F32)
+                yls[h, s] = part.astype(BF16)
+                chain_left(h, s).start()
 
     swap_y(0).wait_recv()
     if FIRST <= NZ - 3:
-        for h in pieces:
-            chain_step(h, 0)
+        chain_step(0, True)
         down(0, FIRST)
-        go(swap_y(1))
+        swap_y(1).start()
+        chain_step(0, False)
         swap_y(1).wait_recv()
     else:
         down(0, FIRST)
-        go(swap_y(1))
+        swap_y(1).start()
         swap_y(1).wait_recv()
-        for h in pieces:
-            chain_step(h, 0)
+        chain_step(0, True)
+        chain_step(0, False)
     for s in range(1, far):
-        for h in pieces:
-            chain_step(h, s)
+        chain_step(s, True)
+        chain_step(s, False)
+
     def returned(k):
         return remote(ret_s.at[k], ret_r.at[e], rs_sem.at[0], rr_sem.at[0], (d, k))
 
@@ -507,45 +523,53 @@
     final = stream_v[...].astype(F32) + dot(dhi_v[...], back_rows) + dot(dlo_v[...], back_rows)
     outg[c, z] = final.astype(BF16)
 
-    def send_out(i):
-        p = (z + i) % NZ
-        return remote(outg.at[c, z], outg.at[c, z], os_sem.at[0], or_sem.at[z], (2 * p + c, e))
-
-    def wait_out(i):
-        p = (z + NZ - i) % NZ
-        remote(outg.at[c, p], outg.at[c, p], os_sem.at[i], or_sem.at[p], (2 * p + c, e)).wait_recv()
+    def send_out(off):
+        return remote(outg.at[c, z], outg.at[c, z], os_sem.at[0], or_sem.at[z], (2 * ((z + off) % NZ) + c, e))
+
+    def wait_out(p):
+        remote(outg.at[c, p], outg.at[c, p], os_sem.at[0], or_sem.at[p], (2 * z + c, e)).wait_recv()
 
     def pass_out(p):
         return remote(outg.at[c, p], outg.at[c, p], ts_sem.at[0], tr_sem.at[p], sibling)
 
-    times(1, NZ, lambda i: send_out(i).start())
-    all_sent(outg.at[0, pl.ds(0, NZ - 1)], os_sem, or_sem)
+    near = [off for k in range(far - 1, 0, -1) for off in (k, NZ - k)]
+    for off in near:
+        send_out(off).start()
     pass_out(z).start()
+    all_sent(outg.at[0, pl.ds(0, len(near))], os_sem, or_sem)
     all_sent(outg.at[0], ts_sem, tr_sem)
 
-    def relay(i):
-        wait_out(i)
-        pass_out((z + NZ - i) % NZ).start()
-
-    times(1, NZ, relay)
+    def half_way(p, side):
+        part = outg.at[c, p, pl.ds(side * ROWS, ROWS)]
+        return remote(part, part, fs_sem.at[0], fr_sem.at[side], (right, left)[side])
+
+    for off in near:
+        p = (z + off) % NZ
+        wait_out(p)
+        if off == NZ - (far - 1):
+            half_way(p, 0).start()
+        if off == far - 1:
+            half_way(p, 1).start()
+        pass_out(p).start()
+    last = ahead_z(far)
+    all_sent(outg.at[0, 0], fs_sem, fr_sem)
+    for side in range(2):
+        half_way(last, side).wait_recv()
+    pass_out(last).start()
 
     def store_out(m, p):
         at = layer_out.at[pl.ds(pl.multiple_of(p * LW, LW), LW), pl.ds(pl.multiple_of(m * LANES, LANES), LANES)]
-        return pltpu.make_async_copy(outg.at[m, p], at, out_sem.at[m, p])
-
-    def wait_pass(i):
-        p = (z + NZ - i) % NZ
-        remote(outg.at[1 - c, p], outg.at[1 - c, p], ts_sem.at[p], tr_sem.at[p], sibling).wait_recv()
+        return pltpu.make_async_copy(outg.at[m, p], at, out_sem.at[0])
+
+    def wait_pass(p):
+        remote(outg.at[1 - c, p], outg.at[1 - c, p], ts_sem.at[0], tr_sem.at[p], sibling).wait_recv()
         store_out(c, p).start()
         store_out(1 - c, p).start()
 
-    times(0, NZ, wait_pass)
-
-    def stored(p):
-        store_out(c, p).wait()
-        store_out(1 - c, p).wait()
-
-    times(0, NZ, stored)
+    for off in [0, *near, far]:
+        wait_pass((z + off) % NZ)
+
+    pltpu.make_async_copy(outg, outg, out_sem.at[0]).wait()
 
     for wait in ending:
         wait()
@@ -603,12 +627,12 @@
         V((NP, far, HE, PC, LANES), BF16), V((NP, far, HE, PC, LANES), BF16),
         V((NE, PC, LANES), BF16), V((NE, PC, LANES), BF16),
         V((NE * PC, LW), BF16), V((LW, NE * PC), BF16), V((LW, NE * PC), BF16), V((2, NZ, LW, LANES), BF16),
-        S((20,)), S((NE,)), S((NE,)), S((NE,)), S((NE,)), S((2,)),
-        S((2 * NZ,)), S((2 * NZ,)), S((2 * NZ,)), S((2 * NZ,)), S((NE,)), S((NE,)),
-        S((NZ,)), S((NZ,)), S((NZ,)), S((NZ,)), S((NE,)), S((NE,)),
-        S((NP, far)), S((NP, far)), S((NP, far)), S((NP, far)), S((NZ,)), S((NZ,)),
-        S((2,)), S((2,)), S((NP, far)), S((NP, far)), S((NP, far)), S((NP, far)),
-        S((NE,)), S((NE,)), S((NZ,)), S((NZ,)), S((NZ,)), S((NZ,)), S((2, NZ)),
+        S((20,)), S((1,)), S((1,)), S((1,)), S((1,)), S((2,)),
+        S((1,)), S((1,)), S((1,)), S((1,)), S((1,)), S((NE,)),
+        S((1,)), S((1,)), S((1,)), S((NZ,)), S((1,)), S((1,)),
+        S((1,)), S((NP, far)), S((NP, far)), S((1,)), S((NZ,)),
+        S((1,)), S((2,)), S((1,)), S((NP, far)), S((NP, far)),
+        S((1,)), S((1,)), S((1,)), S((NZ,)), S((1,)), S((NZ,)), S((1,)), S((1,)), S((2,)),
     ]
     call = pl.pallas_call(
         functools.partial(kernel, (NE, NZ, ROWS, MC, CAP)),

time: 121 us -> 117 us (0.967)
  Pallas kernels: 121 us -> 116 us
    pallas_call x1, Pallas kernels: 119 us -> 114 us  [body(): call(ssm_state, conv_state.transpose(1, 0, 2), new_slot.reshape(NZ, LW),...]
where the time goes in v3:
time: 117 us; the launch traced here: 116 us
  Pallas kernels  116 us (99%)
    pallas_call x1, Pallas kernels, body(): call(ssm_state, conv_state.transpose(1, 0, 2), new_slot.reshape(NZ, LW),...  114 us

profile of v3, /device:TPU:1, one launch (start us, length us, event | category | flops | bytes accessed | tf_op | source)
XLA Modules:
  0.0 116.5 jit_solution(6254854779373403455)
XLA Ops:
  0.6 113.8 %decode_step.1 = (bf16[64,16,256]{2,1,0:T(8,128)(2,1)}, bf16[3,64,256]{2,1,0:T(8,128)(2,1)}, bf16[1024,256]{1,0:T(8,128)(2,1)}) custom-call(bf16[64,16,256]{2,1,0:T(8,128)(2,1)} %ssm_hbm.1, bf16[3,64,256]{2,1,0:T(8,128)(2,1)} %bitcast.21, s32[8,128]{1,0:T(8,128)} %bitcast.25, bf16[64,256]{1,0:T(8,128)(2,1)} %cin_hbm.1, bf16[64,256]{1,0:T(8,128)(2,1)} %gin_hbm.1, ...), custom_call_target="tpu_custom_call" | custom-call | tf_op jit(solution)/shard_map/decode_step/pallas_call | solution.py:652
  114.4 2.1 %hand_over.1 = (bf16[64,16,256]{2,1,0:T(8,128)(2,1)}, bf16[3,64,256]{2,1,0:T(8,128)(2,1)}, bf16[1024,256]{1,0:T(8,128)(2,1)}) custom-call(bf16[64,16,256]{2,1,0:T(8,128)(2,1)} %get-tuple-element.9.a, bf16[3,64,256]{2,1,0:T(8,128)(2,1)} %get-tuple-element.10.b, bf16[1024,256]{1,0:T(8,128)(2,1)} %get-tuple-element.11.c), custom_call_target="tpu_custom_call" | custom-call | tf_op jit(solution)/shard_map/hand_over/pallas_call | solution.py:659

commit v4 on v3

--- a/solution.py
+++ b/solution.py
@@ -375,7 +375,7 @@
     steps.append([(NZ - 1, ahead_z(far), far)])
     number = {off % NZ: o for group in steps for o, _, off in group}
     FIRST = sum(len(group) for group in steps[: max(1, far - 1)])
-    KC = min(D, 1024)
+    KC = min(D, 2048)
 
     def gate_up(lo, hi):
         rows = pl.ds(lo * MP, (hi - lo) * MP)

time: 117 us -> 116 us (level)
  no operation moved by 1% of the time
where the time goes in v4:
time: 116 us
  Pallas kernels  115 us (99%)
    pallas_call x1, Pallas kernels, body(): call(ssm_state, conv_state.transpose(1, 0, 2), new_slot.reshape(NZ, LW),...  113 us

profile of v4, /device:TPU:1, one launch (start us, length us, event | category | flops | bytes accessed | tf_op | source)
XLA Modules:
  0.0 115.7 jit_solution(5759169871532858436)
XLA Ops:
  0.6 113.0 %decode_step.1 = (bf16[64,16,256]{2,1,0:T(8,128)(2,1)}, bf16[3,64,256]{2,1,0:T(8,128)(2,1)}, bf16[1024,256]{1,0:T(8,128)(2,1)}) custom-call(bf16[64,16,256]{2,1,0:T(8,128)(2,1)} %ssm_hbm.1, bf16[3,64,256]{2,1,0:T(8,128)(2,1)} %bitcast.21, s32[8,128]{1,0:T(8,128)} %bitcast.25, bf16[64,256]{1,0:T(8,128)(2,1)} %cin_hbm.1, bf16[64,256]{1,0:T(8,128)(2,1)} %gin_hbm.1, ...), custom_call_target="tpu_custom_call" | custom-call | tf_op jit(solution)/shard_map/decode_step/pallas_call | solution.py:652
  113.7 2.1 %hand_over.1 = (bf16[64,16,256]{2,1,0:T(8,128)(2,1)}, bf16[3,64,256]{2,1,0:T(8,128)(2,1)}, bf16[1024,256]{1,0:T(8,128)(2,1)}) custom-call(bf16[64,16,256]{2,1,0:T(8,128)(2,1)} %get-tuple-element.9.a, bf16[3,64,256]{2,1,0:T(8,128)(2,1)} %get-tuple-element.10.b, bf16[1024,256]{1,0:T(8,128)(2,1)} %get-tuple-element.11.c), custom_call_target="tpu_custom_call" | custom-call | tf_op jit(solution)/shard_map/hand_over/pallas_call | solution.py:659
